TPU v7x, 32 devices: a whole 2x2x4 slice. The times are simulated.
32 devices in a mesh: fsdp: 8 (over z, x), tensor: 4 (over y, core).
Axes of the slice: x: 2, y: 2, z: 4, core: 2. Of those that a mesh axis runs over, the one named last changes fastest.
Arguments:
- hidden_in: bfloat16 [8192, 768], P(('fsdp', 'tensor')), may hold values from -6 to 6
- time_embed: bfloat16 [8, 768], P('fsdp'), may hold values from -6 to 6
- segment_ids: int32 [8, 1024], P('fsdp'), may hold values from -1 to 7, as said below
- cotangent: bfloat16 [8192, 768], P(('fsdp', 'tensor')), may hold values from -6 to 6
- query_weight: bfloat16 [2, 768, 768], P(None, 'fsdp', 'tensor'), may hold values from -0.21875 to 0.21875
- key_weight: bfloat16 [2, 768, 768], P(None, 'fsdp', 'tensor'), may hold values from -0.21875 to 0.21875
- value_weight: bfloat16 [2, 768, 768], P(None, 'fsdp', 'tensor'), may hold values from -0.21875 to 0.21875
- output_weight: bfloat16 [2, 768, 768], P(None, 'tensor', 'fsdp'), may hold values from -1.75 to 1.75
- up_weight: bfloat16 [2, 768, 3072], P(None, 'fsdp', 'tensor'), may hold values from -0.21875 to 0.21875
- down_weight: bfloat16 [2, 3072, 768], P(None, 'tensor', 'fsdp'), may hold values from -0.109375 to 0.109375
- query_bias: float32 [2, 768], P(None, 'tensor'), may hold values from -3 to 3
- value_bias: float32 [2, 768], P(None, 'tensor'), may hold values from -3 to 3
- output_bias: float32 [2, 768], replicated, may hold values from -3 to 3
- up_bias: float32 [2, 3072], P(None, 'tensor'), may hold values from -3 to 3
- down_bias: float32 [2, 768], replicated, may hold values from -3 to 3
- first_gain: float32 [2, 768], replicated, may hold values from 0.25 to 1.75
- first_shift: float32 [2, 768], replicated, may hold values from -3 to 3
- second_gain: float32 [2, 768], replicated, may hold values from 0.25 to 1.75
- second_shift: float32 [2, 768], replicated, may hold values from -3 to 3
Outputs:
- denoised: bfloat16 [8192, 768], P(('fsdp', 'tensor'))
- input_grad: float32 [8192, 768], P(('fsdp', 'tensor'))
- query_weight_grad: float32 [2, 768, 768], P(None, 'fsdp', 'tensor')
- key_weight_grad: float32 [2, 768, 768], P(None, 'fsdp', 'tensor')
- value_weight_grad: float32 [2, 768, 768], P(None, 'fsdp', 'tensor')
- output_weight_grad: float32 [2, 768, 768], P(None, 'tensor', 'fsdp')
- up_weight_grad: float32 [2, 768, 3072], P(None, 'fsdp', 'tensor')
- down_weight_grad: float32 [2, 3072, 768], P(None, 'tensor', 'fsdp')
- query_bias_grad: float32 [2, 768], P(None, 'tensor')
- value_bias_grad: float32 [2, 768], P(None, 'tensor')
- output_bias_grad: float32 [2, 768], replicated
- up_bias_grad: float32 [2, 3072], P(None, 'tensor')
- down_bias_grad: float32 [2, 768], replicated
- first_gain_grad: float32 [2, 768], replicated
- first_shift_grad: float32 [2, 768], replicated
- second_gain_grad: float32 [2, 768], replicated
- second_shift_grad: float32 [2, 768], replicated
Inputs may be any that keep to these rules, and one draw needn't show every extreme that they name: `segment_ids`: each sequence holds 8 documents of at least one token in order 0 to 7, followed by padding of at least one token.
All inputs are finite; a program needn't handle non-finite values.
Results may differ from a plain program's by a relative error of at most 0.015.
Values may be sent and summed in bfloat16 or wider, within the bound.
No kernel may reach another device: no remote copies, remote signals or barrier semaphores. Data moves between devices by JAX's collectives and lax.ppermute only.
A program may use at most 192 MiB of HBM per device.

v0:
```python
import jax
import jax.numpy as jnp
from jax import lax
from jax.sharding import PartitionSpec as P

HEAD_DIM = 64


EPSILON = 1e-05


def apply_layer_norm(token_rows, gain, shift):
    center = token_rows - jnp.mean(token_rows, axis=1, keepdims=True)
    factor = lax.rsqrt(jnp.mean(center * center, axis=1, keepdims=True) + EPSILON)
    normed = center * factor
    return (normed * gain + shift, normed, factor)


def norm_backward(grad_normed, normed, factor, gain):
    scaled = grad_normed * gain
    grad_input = factor * (
        scaled
        - jnp.mean(scaled, axis=1, keepdims=True)
        - normed * jnp.mean(scaled * normed, axis=1, keepdims=True)
    )
    return (jnp.sum(grad_normed * normed, axis=0), jnp.sum(grad_normed, axis=0), grad_input)


def fetch(matrices, layer):
    pieces = tuple((part[layer] for part in matrices))
    return (
        lax.all_gather(pieces[0], "fsdp", axis=0, tiled=True),
        lax.all_gather(pieces[1], "fsdp", axis=0, tiled=True),
        lax.all_gather(pieces[2], "fsdp", axis=0, tiled=True),
        lax.all_gather(pieces[3], "fsdp", axis=1, tiled=True),
        lax.all_gather(pieces[4], "fsdp", axis=0, tiled=True),
        lax.all_gather(pieces[5], "fsdp", axis=1, tiled=True),
    )


def spread(normed_low):
    return lax.all_gather(normed_low, "tensor", axis=0, tiled=True)


def collect(partial_rows):
    return lax.psum_scatter(partial_rows, "tensor", scatter_dimension=0, tiled=True)


def spread_grad(grad_low):
    return lax.all_gather(grad_low, "tensor", axis=0, tiled=True)


def collect_grad(partial_rows):
    return lax.psum_scatter(partial_rows, "tensor", scatter_dimension=0, tiled=True)


def sum_weights(grads):
    return (
        lax.psum_scatter(grads[0], "fsdp", scatter_dimension=0, tiled=True),
        lax.psum_scatter(grads[1], "fsdp", scatter_dimension=0, tiled=True),
        lax.psum_scatter(grads[2], "fsdp", scatter_dimension=0, tiled=True),
        lax.psum_scatter(grads[3], "fsdp", scatter_dimension=1, tiled=True),
        lax.psum_scatter(grads[4], "fsdp", scatter_dimension=0, tiled=True),
        lax.psum_scatter(grads[5], "fsdp", scatter_dimension=1, tiled=True),
    )


def gelu_tanh(values):
    return jax.nn.gelu(values, approximate=True)


def layer_forward(token_rows, weights, vectors, same_doc, head_dim):
    query_w, key_w, value_w, out_w, up_w, down_w = weights
    (
        query_b,
        value_b,
        out_b,
        up_b,
        down_b,
        norm_gain_first,
        norm_offset_first,
        norm_gain_second,
        norm_offset_second,
    ) = vectors
    normalized_first, centered_unit_first, inverse_scale_first = apply_layer_norm(
        token_rows, norm_gain_first, norm_offset_first
    )
    first = spread(normalized_first.astype(jnp.bfloat16))
    length = first.shape[0]
    query = (jnp.dot(first, query_w, preferred_element_type=jnp.float32) + query_b).astype(
        jnp.bfloat16
    )
    key = jnp.dot(first, key_w, preferred_element_type=jnp.float32).astype(jnp.bfloat16)
    value = (jnp.dot(first, value_w, preferred_element_type=jnp.float32) + value_b).astype(
        jnp.bfloat16
    )
    query = query.reshape(length, -1, head_dim)
    key = key.reshape(length, -1, head_dim)
    value = value.reshape(length, -1, head_dim)
    scores = jnp.einsum(
        "qhd,khd->hqk", query, key, preferred_element_type=jnp.float32
    ) * head_dim ** (-0.5)
    scores = jnp.where(same_doc[None], scores, -jnp.inf)
    top = jnp.max(scores, axis=-1, keepdims=True)
    weights_exp = jnp.exp(scores - top)
    probs = weights_exp / jnp.sum(weights_exp, axis=-1, keepdims=True)
    probs_low = probs.astype(jnp.bfloat16)
    mixed = jnp.einsum("hqk,khd->qhd", probs_low, value, preferred_element_type=jnp.float32)
    mixed = mixed.reshape(length, -1).astype(jnp.bfloat16)
    attended = collect(jnp.dot(mixed, out_w, preferred_element_type=jnp.float32))
    between_layers = token_rows + attended + out_b
    normalized_second, centered_unit_second, inverse_scale_second = apply_layer_norm(
        between_layers, norm_gain_second, norm_offset_second
    )
    second = spread(normalized_second.astype(jnp.bfloat16))
    pre = jnp.dot(second, up_w, preferred_element_type=jnp.float32) + up_b
    act = gelu_tanh(pre).astype(jnp.bfloat16)
    branch = collect(jnp.dot(act, down_w, preferred_element_type=jnp.float32))
    result = between_layers + branch + down_b
    kept = (
        first,
        query,
        key,
        value,
        probs,
        probs_low,
        mixed,
        centered_unit_first,
        inverse_scale_first,
        centered_unit_second,
        inverse_scale_second,
        second,
        pre,
        act,
    )
    return (result, kept)


def layer_backward(grad_out, kept, weights, vectors, head_dim):
    query_w, key_w, value_w, out_w, up_w, down_w = weights
    (
        query_b,
        value_b,
        out_b,
        up_b,
        down_b,
        norm_gain_first,
        norm_offset_first,
        norm_gain_second,
        norm_offset_second,
    ) = vectors
    (
        first,
        query,
        key,
        value,
        probs,
        probs_low,
        mixed,
        centered_unit_first,
        inverse_scale_first,
        centered_unit_second,
        inverse_scale_second,
        second,
        pre,
        act,
    ) = kept
    length = first.shape[0]
    down_b_grad = jnp.sum(grad_out, axis=0)
    full_out = spread_grad(grad_out.astype(jnp.bfloat16))
    down_w_grad = jnp.einsum("rf,rd->fd", act, full_out, preferred_element_type=jnp.float32)
    grad_act = jnp.dot(full_out, down_w.T, preferred_element_type=jnp.float32)
    _, gelu_pull = jax.vjp(gelu_tanh, pre)
    grad_pre = gelu_pull(grad_act)[0].astype(jnp.bfloat16)
    up_b_grad = jnp.sum(grad_pre.astype(jnp.float32), axis=0)
    up_w_grad = jnp.einsum("rd,rf->df", second, grad_pre, preferred_element_type=jnp.float32)
    gradient_later = collect_grad(jnp.dot(grad_pre, up_w.T, preferred_element_type=jnp.float32))
    gain_two_grad, shift_two_grad, through_two = norm_backward(
        gradient_later, centered_unit_second, inverse_scale_second, norm_gain_second
    )
    grad_middle = grad_out + through_two
    out_b_grad = jnp.sum(grad_middle, axis=0)
    full_middle = spread_grad(grad_middle.astype(jnp.bfloat16))
    out_w_grad = jnp.einsum("re,rd->ed", mixed, full_middle, preferred_element_type=jnp.float32)
    grad_mixed = jnp.dot(full_middle, out_w.T, preferred_element_type=jnp.float32).astype(
        jnp.bfloat16
    )
    grad_mixed = grad_mixed.reshape(length, -1, head_dim)
    grad_value = jnp.einsum(
        "hqk,qhd->khd", probs_low, grad_mixed, preferred_element_type=jnp.float32
    ).astype(jnp.bfloat16)
    grad_probs = jnp.einsum("qhd,khd->hqk", grad_mixed, value, preferred_element_type=jnp.float32)
    row_total = jnp.sum(probs * grad_probs, axis=-1, keepdims=True)
    grad_scores = (probs * (grad_probs - row_total)).astype(jnp.bfloat16)
    scale = head_dim ** (-0.5)
    grad_query = (
        jnp.einsum("hqk,khd->qhd", grad_scores, key, preferred_element_type=jnp.float32) * scale
    ).astype(jnp.bfloat16)
    grad_key = (
        jnp.einsum("hqk,qhd->khd", grad_scores, query, preferred_element_type=jnp.float32) * scale
    ).astype(jnp.bfloat16)
    grad_query = grad_query.reshape(length, -1)
    grad_key = grad_key.reshape(length, -1)
    grad_value = grad_value.reshape(length, -1)
    query_b_grad = jnp.sum(grad_query.astype(jnp.float32), axis=0)
    value_b_grad = jnp.sum(grad_value.astype(jnp.float32), axis=0)
    query_w_grad = jnp.einsum("rd,re->de", first, grad_query, preferred_element_type=jnp.float32)
    key_w_grad = jnp.einsum("rd,re->de", first, grad_key, preferred_element_type=jnp.float32)
    value_w_grad = jnp.einsum("rd,re->de", first, grad_value, preferred_element_type=jnp.float32)
    gradient_earlier = jnp.dot(grad_query, query_w.T, preferred_element_type=jnp.float32)
    gradient_earlier = gradient_earlier + jnp.dot(
        grad_key, key_w.T, preferred_element_type=jnp.float32
    )
    gradient_earlier = gradient_earlier + jnp.dot(
        grad_value, value_w.T, preferred_element_type=jnp.float32
    )
    gradient_earlier = collect_grad(gradient_earlier)
    gain_one_grad, shift_one_grad, through_one = norm_backward(
        gradient_earlier, centered_unit_first, inverse_scale_first, norm_gain_first
    )
    grad_input = grad_middle + through_one
    matrix_grads = (query_w_grad, key_w_grad, value_w_grad, out_w_grad, up_w_grad, down_w_grad)
    vector_grads = (
        query_b_grad,
        value_b_grad,
        out_b_grad,
        up_b_grad,
        down_b_grad,
        gain_one_grad,
        shift_one_grad,
        gain_two_grad,
        shift_two_grad,
    )
    return (grad_input, matrix_grads, vector_grads)


def widen(local_part, position, count):
    width = local_part.shape[0]
    whole = jnp.zeros((width * count,), jnp.float32)
    return lax.dynamic_update_slice_in_dim(whole, local_part, position * width, 0)


def local(
    hidden_in,
    time_embed,
    segment_ids,
    cotangent,
    query_weight,
    key_weight,
    value_weight,
    output_weight,
    up_weight,
    down_weight,
    query_bias,
    value_bias,
    output_bias,
    up_bias,
    down_bias,
    first_gain,
    first_shift,
    second_gain,
    second_shift,
):
    rows_here = hidden_in.shape[0]
    tensor_count = lax.axis_size("tensor")
    position = lax.axis_index("tensor")
    head_dim = HEAD_DIM
    segments = segment_ids[0]
    same_doc = segments[:, None] == segments[None, :]
    local_ids = lax.dynamic_slice_in_dim(segments, position * rows_here, rows_here)
    valid = (local_ids >= 0).astype(jnp.float32)[:, None]
    matrices = (query_weight, key_weight, value_weight, output_weight, up_weight, down_weight)
    layers = query_weight.shape[0]

    def vectors_of(layer):
        return (
            query_bias[layer],
            value_bias[layer],
            output_bias[layer],
            up_bias[layer],
            down_bias[layer],
            first_gain[layer],
            first_shift[layer],
            second_gain[layer],
            second_shift[layer],
        )

    current = hidden_in.astype(jnp.float32) + time_embed.astype(jnp.float32)
    inputs = []
    fetched = []
    for layer in range(layers):
        weights = fetch(matrices, layer)
        fetched.append(weights)
        inputs.append(current)
        current = layer_forward(current, weights, vectors_of(layer), same_doc, head_dim)[0]
    denoised = current.astype(jnp.bfloat16)
    grad = cotangent.astype(jnp.float32) * valid
    matrix_shards = [None] * layers
    vector_rows = [None] * layers
    up_rows = [None] * layers
    for layer in reversed(range(layers)):
        weights = fetch(matrices, layer)
        kept = layer_forward(inputs[layer], weights, vectors_of(layer), same_doc, head_dim)[1]
        grad, matrix_grads, vector_grads = layer_backward(
            grad, kept, weights, vectors_of(layer), head_dim
        )
        matrix_shards[layer] = sum_weights(matrix_grads)
        (
            query_b_grad,
            value_b_grad,
            out_b_grad,
            up_b_grad,
            down_b_grad,
            gain_one_grad,
            shift_one_grad,
            gain_two_grad,
            shift_two_grad,
        ) = vector_grads
        vector_rows[layer] = jnp.stack(
            [
                gain_one_grad,
                shift_one_grad,
                gain_two_grad,
                shift_two_grad,
                out_b_grad,
                down_b_grad,
                widen(query_b_grad, position, tensor_count),
                widen(value_b_grad, position, tensor_count),
            ]
        )
        up_rows[layer] = widen(up_b_grad, position, tensor_count)
    vector_total, up_total = lax.psum(
        (jnp.stack(vector_rows), jnp.stack(up_rows)), ("fsdp", "tensor")
    )
    stacked = [
        jnp.stack([matrix_shards[layer][index] for layer in range(layers)]) for index in range(6)
    ]
    width_here = query_bias.shape[1]
    hidden_here = up_bias.shape[1]
    query_b_out = lax.dynamic_slice_in_dim(
        vector_total[:, 6, :], position * width_here, width_here, 1
    )
    value_b_out = lax.dynamic_slice_in_dim(
        vector_total[:, 7, :], position * width_here, width_here, 1
    )
    up_b_out = lax.dynamic_slice_in_dim(up_total, position * hidden_here, hidden_here, 1)
    return (
        denoised,
        grad,
        stacked[0],
        stacked[1],
        stacked[2],
        stacked[3],
        stacked[4],
        stacked[5],
        query_b_out,
        value_b_out,
        vector_total[:, 4, :],
        up_b_out,
        vector_total[:, 5, :],
        vector_total[:, 0, :],
        vector_total[:, 1, :],
        vector_total[:, 2, :],
        vector_total[:, 3, :],
    )


def solution(mesh):
    in_specs = (
        P(("fsdp", "tensor"), None),
        P("fsdp", None),
        P("fsdp", None),
        P(("fsdp", "tensor"), None),
        P(None, "fsdp", "tensor"),
        P(None, "fsdp", "tensor"),
        P(None, "fsdp", "tensor"),
        P(None, "tensor", "fsdp"),
        P(None, "fsdp", "tensor"),
        P(None, "tensor", "fsdp"),
        P(None, "tensor"),
        P(None, "tensor"),
        P(),
        P(None, "tensor"),
        P(),
        P(),
        P(),
        P(),
        P(),
    )
    out_specs = (
        P(("fsdp", "tensor"), None),
        P(("fsdp", "tensor"), None),
        P(None, "fsdp", "tensor"),
        P(None, "fsdp", "tensor"),
        P(None, "fsdp", "tensor"),
        P(None, "tensor", "fsdp"),
        P(None, "fsdp", "tensor"),
        P(None, "tensor", "fsdp"),
        P(None, "tensor"),
        P(None, "tensor"),
        P(),
        P(None, "tensor"),
        P(),
        P(),
        P(),
        P(),
        P(),
    )
    return jax.shard_map(local, mesh=mesh, in_specs=in_specs, out_specs=out_specs, check_vma=False)
```

profile of v0, /device:TPU:0, one launch (start us, length us, event | category | flops | bytes accessed | tf_op | source)
XLA Modules:
  0.0 1855.5 jit_solution(11770342703891644746)
XLA Ops:
  16.0 33.8 %all-gather.3 = bf16[1,192,768]{1,0,2:T(2,128)(2,1)S(1)} all-gather(bf16[1,192,96]{1,0,2:T(2,128)(2,1)S(1)} %copy.81), channel_id=5, replica_groups=mesh['fsdp'=8,'tensor'=4] {'fsdp'}, dimensions={2}, use_global_device_ids=true | all-gather | bytes 331776 | tf_op jit(solution)/shard_map/all_gather | solution.py:35
  50.9 31.2 %all-gather = bf16[1,768,192]{2,1,0:T(8,128)(2,1)S(1)} all-gather(bf16[1,96,192]{2,1,0:T(8,128)(2,1)S(1)} %get-tuple-element.74), channel_id=2, replica_groups=mesh['fsdp'=8,'tensor'=4] {'fsdp'}, dimensions={1}, use_global_device_ids=true | all-gather | bytes 331776 | tf_op jit(solution)/shard_map/all_gather | solution.py:34
  82.8 31.1 %all-gather.2 = bf16[1,768,192]{2,1,0:T(8,128)(2,1)S(1)} all-gather(bf16[1,96,192]{2,1,0:T(8,128)(2,1)S(1)} %get-tuple-element.70), channel_id=4, replica_groups=mesh['fsdp'=8,'tensor'=4] {'fsdp'}, dimensions={1}, use_global_device_ids=true | all-gather | bytes 331776 | tf_op jit(solution)/shard_map/all_gather | solution.py:33
  114.6 31.0 %all-gather.1 = bf16[1,768,192]{2,1,0:T(8,128)(2,1)S(1)} all-gather(bf16[1,96,192]{2,1,0:T(8,128)(2,1)S(1)} %get-tuple-element.72), channel_id=3, replica_groups=mesh['fsdp'=8,'tensor'=4] {'fsdp'}, dimensions={1}, use_global_device_ids=true | all-gather | bytes 331776 | tf_op jit(solution)/shard_map/all_gather | solution.py:32
  173.2 36.9 %reduce-scatter.25.cloned.1.call-done = f32[256,768]{1,0:T(8,128)} async-done(((f32[1024,768]{1,0:T(8,128)}), f32[256,768]{1,0:T(8,128)}) %reduce-scatter.25.cloned.1.call-update) | async-done | bytes 786448 | tf_op jit(solution)/shard_map/reduce_scatter | solution.py:46
  217.0 20.1 %all-gather.27.cloned.1.call-done = bf16[1024,768]{1,0:T(8,128)(2,1)} async-done(((bf16[256,768]{1,0:T(8,128)(2,1)}), bf16[1024,768]{1,0:T(8,128)(2,1)}) %all-gather.27.cloned.1.call-update) | async-done | bytes 1572880 | tf_op jit(solution)/shard_map/all_gather | solution.py:42
  241.9 39.6 %all-gather.43.cloned.1.call-done = bf16[1,768,768]{1,2,0:T(8,128)(2,1)} async-done(((bf16[1,768,96]{1,2,0:T(8,128)(2,1)}), bf16[1,768,768]{1,2,0:T(8,128)(2,1)}) %all-gather.43.cloned.1.call-update) | async-done | bytes 1179664 | tf_op jit(solution)/shard_map/all_gather | solution.py:37
  288.7 35.2 %reduce-scatter.27.cloned.1.call-done = f32[256,768]{1,0:T(8,128)} async-done(((f32[1024,768]{1,0:T(8,128)}), f32[256,768]{1,0:T(8,128)}) %reduce-scatter.27.cloned.1.call-update) | async-done | bytes 786448 | tf_op jit(solution)/shard_map/reduce_scatter | solution.py:46
  326.6 32.2 %all-gather.9 = bf16[1,192,768]{1,0,2:T(2,128)(2,1)S(1)} all-gather(bf16[1,192,96]{1,0,2:T(2,128)(2,1)S(1)} %copy.82), channel_id=11, replica_groups=mesh['fsdp'=8,'tensor'=4] {'fsdp'}, dimensions={2}, use_global_device_ids=true | all-gather | bytes 331776 | tf_op jit(solution)/shard_map/all_gather | solution.py:35
  360.5 31.2 %all-gather.6 = bf16[1,768,192]{2,1,0:T(8,128)(2,1)S(1)} all-gather(bf16[1,96,192]{2,1,0:T(8,128)(2,1)S(1)} %copy-done.47), channel_id=8, replica_groups=mesh['fsdp'=8,'tensor'=4] {'fsdp'}, dimensions={1}, use_global_device_ids=true | all-gather | bytes 331776 | tf_op jit(solution)/shard_map/all_gather | solution.py:34
  391.7 31.0 %all-gather.8 = bf16[1,768,192]{2,1,0:T(8,128)(2,1)S(1)} all-gather(bf16[1,96,192]{2,1,0:T(8,128)(2,1)S(1)} %copy-done.48), channel_id=10, replica_groups=mesh['fsdp'=8,'tensor'=4] {'fsdp'}, dimensions={1}, use_global_device_ids=true | all-gather | bytes 331776 | tf_op jit(solution)/shard_map/all_gather | solution.py:33
  422.6 31.0 %all-gather.7 = bf16[1,768,192]{2,1,0:T(8,128)(2,1)S(1)} all-gather(bf16[1,96,192]{2,1,0:T(8,128)(2,1)S(1)} %copy-done.49), channel_id=9, replica_groups=mesh['fsdp'=8,'tensor'=4] {'fsdp'}, dimensions={1}, use_global_device_ids=true | all-gather | bytes 331776 | tf_op jit(solution)/shard_map/all_gather | solution.py:32
  482.0 37.4 %reduce-scatter.29.cloned.1.call-done = f32[256,768]{1,0:T(8,128)} async-done(((f32[1024,768]{1,0:T(8,128)}), f32[256,768]{1,0:T(8,128)}) %reduce-scatter.29.cloned.1.call-update) | async-done | bytes 786448 | tf_op jit(solution)/shard_map/reduce_scatter | solution.py:46
  526.8 20.1 %all-gather.31.cloned.1.call-done = bf16[1024,768]{1,0:T(8,128)(2,1)} async-done(((bf16[256,768]{1,0:T(8,128)(2,1)}), bf16[1024,768]{1,0:T(8,128)(2,1)}) %all-gather.31.cloned.1.call-update) | async-done | bytes 1572880 | tf_op jit(solution)/shard_map/all_gather | solution.py:42
  551.8 39.5 %all-gather.47.cloned.1.call-done = bf16[1,768,768]{1,2,0:T(8,128)(2,1)} async-done(((bf16[1,768,96]{1,2,0:T(8,128)(2,1)}), bf16[1,768,768]{1,2,0:T(8,128)(2,1)}) %all-gather.47.cloned.1.call-update) | async-done | bytes 1179664 | tf_op jit(solution)/shard_map/all_gather | solution.py:37
  627.7 31.9 %reduce-scatter.33.cloned.1.call-done = f32[256,768]{1,0:T(8,128)} async-done(((f32[1024,768]{1,0:T(8,128)}), f32[256,768]{1,0:T(8,128)}) %reduce-scatter.33.cloned.1.call-update) | async-done | bytes 786448 | tf_op jit(solution)/shard_map/reduce_scatter | solution.py:54
  662.6 37.4 %reduce-scatter.31.cloned.1.call-done = f32[256,768]{1,0:T(8,128)} async-done(((f32[1024,768]{1,0:T(8,128)}), f32[256,768]{1,0:T(8,128)}) %reduce-scatter.31.cloned.1.call-update) | async-done | bytes 786448 | tf_op jit(solution)/shard_map/reduce_scatter | solution.py:46
  755.0 37.9 %reduce-scatter.35.cloned.1.call-done = f32[256,768]{1,0:T(8,128)} async-done(((f32[1024,768]{1,0:T(8,128)}), f32[256,768]{1,0:T(8,128)}) %reduce-scatter.35.cloned.1.call-update) | async-done | bytes 786448 | tf_op jit(solution)/shard_map/reduce_scatter | solution.py:54
  830.7 37.9 %reduce-scatter.37.cloned.1.call-done = f32[256,768]{1,0:T(8,128)} async-done(((f32[1024,768]{1,0:T(8,128)}), f32[256,768]{1,0:T(8,128)}) %reduce-scatter.37.cloned.1.call-update) | async-done | bytes 786448 | tf_op jit(solution)/shard_map/reduce_scatter | solution.py:54
  949.5 63.5 %reduce-scatter.59.cloned.1.call-done = f32[768,96]{0,1:T(8,128)} async-done(((f32[768,768]{0,1:T(8,128)}), f32[768,96]{0,1:T(8,128)}) %reduce-scatter.59.cloned.1.call-update) | async-done | bytes 294928 | tf_op jit(solution)/shard_map/reduce_scatter | solution.py:64
  1013.0 71.5 %reduce-scatter.57.cloned.1.call-done = f32[768,96]{0,1:T(8,128)} async-done(((f32[768,768]{0,1:T(8,128)}), f32[768,96]{0,1:T(8,128)}) %reduce-scatter.57.cloned.1.call-update) | async-done | bytes 294928 | tf_op jit(solution)/shard_map/reduce_scatter | solution.py:64
  1086.4 69.8 %reduce-scatter.55.cloned.1.call-done = f32[96,768]{1,0:T(8,128)} async-done(((f32[768,768]{1,0:T(8,128)}), f32[96,768]{1,0:T(8,128)}) %reduce-scatter.55.cloned.1.call-update) | async-done | bytes 294928 | tf_op jit(solution)/shard_map/reduce_scatter | solution.py:63
  1156.2 71.7 %reduce-scatter.53.cloned.1.call-done = f32[96,768]{1,0:T(8,128)} async-done(((f32[768,768]{1,0:T(8,128)}), f32[96,768]{1,0:T(8,128)}) %reduce-scatter.53.cloned.1.call-update) | async-done | bytes 294928 | tf_op jit(solution)/shard_map/reduce_scatter | solution.py:63
  1230.3 62.6 %reduce-scatter.61.cloned.1.call-done = f32[96,192]{1,0:T(8,128)} async-done(((f32[768,192]{1,0:T(8,128)}), f32[96,192]{1,0:T(8,128)}) %reduce-scatter.61.cloned.1.call-update) | async-done | bytes 73744
  1294.6 63.6 %reduce-scatter.51.cloned.1.call-done = f32[96,192]{1,0:T(8,128)} async-done(((f32[768,192]{1,0:T(8,128)}), f32[96,192]{1,0:T(8,128)}) %reduce-scatter.51.cloned.1.call-update) | async-done | bytes 73744 | tf_op jit(solution)/shard_map/reduce_scatter | solution.py:61
  1358.2 64.8 %reduce-scatter.49.cloned.1.call-done = f32[96,192]{1,0:T(8,128)} async-done(((f32[768,192]{1,0:T(8,128)}), f32[96,192]{1,0:T(8,128)}) %reduce-scatter.49.cloned.1.call-update) | async-done | bytes 73744 | tf_op jit(solution)/shard_map/reduce_scatter | solution.py:61
  1424.6 63.6 %reduce-scatter.47.cloned.1.call-done = f32[96,192]{1,0:T(8,128)} async-done(((f32[768,192]{1,0:T(8,128)}), f32[96,192]{1,0:T(8,128)}) %reduce-scatter.47.cloned.1.call-update) | async-done | bytes 73744 | tf_op jit(solution)/shard_map/reduce_scatter | solution.py:60
  1488.3 64.8 %reduce-scatter.45.cloned.1.call-done = f32[96,192]{1,0:T(8,128)} async-done(((f32[768,192]{1,0:T(8,128)}), f32[96,192]{1,0:T(8,128)}) %reduce-scatter.45.cloned.1.call-update) | async-done | bytes 73744 | tf_op jit(solution)/shard_map/reduce_scatter | solution.py:60
  1554.7 63.5 %reduce-scatter.43.cloned.1.call-done = f32[96,192]{1,0:T(8,128)} async-done(((f32[768,192]{1,0:T(8,128)}), f32[96,192]{1,0:T(8,128)}) %reduce-scatter.43.cloned.1.call-update) | async-done | bytes 73744 | tf_op jit(solution)/shard_map/reduce_scatter | solution.py:59
  1618.2 64.8 %reduce-scatter.41.cloned.1.call-done = f32[96,192]{1,0:T(8,128)} async-done(((f32[768,192]{1,0:T(8,128)}), f32[96,192]{1,0:T(8,128)}) %reduce-scatter.41.cloned.1.call-update) | async-done | bytes 73744 | tf_op jit(solution)/shard_map/reduce_scatter | solution.py:59
  1684.7 37.9 %reduce-scatter.39.cloned.1.call-done = f32[256,768]{1,0:T(8,128)} async-done(((f32[1024,768]{1,0:T(8,128)}), f32[256,768]{1,0:T(8,128)}) %reduce-scatter.39.cloned.1.call-update) | async-done | bytes 786448 | tf_op jit(solution)/shard_map/reduce_scatter | solution.py:54
  1727.4 116.5 %all-reduce.3.cloned.1.call-done = (f32[2,8,768]{2,0,1:T(2,128)}, f32[2,3072]{1,0:T(2,128)}) async-done(((f32[2,8,768]{2,0,1:T(2,128)}, f32[2,3072]{1,0:T(2,128)}), (f32[2,8,768]{2,0,1:T(2,128)}, f32[2,3072]{1,0:T(2,128)})) %all-reduce.3.cloned.1.call-update) | async-done | bytes 73744 | tf_op jit(solution)/shard_map/psum | solution.py:332
  (451 shorter events, 333.0 us)
Async XLA Ops:
  8.1 140.3 %all-gather.25.cloned.1.call-start = ((), (), s32[]{:S(2)}) async-start(), calls=%async_computation.20 | async-start | bytes 1966080 | tf_op jit(solution)/shard_map/all_gather | solution.py:42
  14.9 195.1 %reduce-scatter.25.cloned.1.call-start = ((), (), s32[]{:S(2)}) async-start(), calls=%async_computation.21 | async-start | bytes 3932160 | tf_op jit(solution)/shard_map/reduce_scatter | solution.py:46
  171.1 45.9 %all-gather.41.cloned.1.call-start = ((), (), s32[]{:S(2)}) async-start(), calls=%async_computation.46 | async-start | bytes 1327104 | tf_op jit(solution)/shard_map/all_gather | solution.py:36
  171.9 65.2 %all-gather.27.cloned.1.call-start = ((), (), s32[]{:S(2)}) async-start(), calls=%async_computation.22 | async-start | bytes 1966080 | tf_op jit(solution)/shard_map/all_gather | solution.py:42
  212.6 68.8 %all-gather.43.cloned.1.call-start = ((), (), s32[]{:S(2)}) async-start(), calls=%async_computation.47 | async-start | bytes 1327104 | tf_op jit(solution)/shard_map/all_gather | solution.py:37
  213.5 110.4 %reduce-scatter.27.cloned.1.call-start = ((), (), s32[]{:S(2)}) async-start(), calls=%async_computation.23 | async-start | bytes 3932160 | tf_op jit(solution)/shard_map/reduce_scatter | solution.py:46
  287.4 166.1 %all-gather.29.cloned.1.call-start = ((), (), s32[]{:S(2)}) async-start(), calls=%async_computation.24 | async-start | bytes 1966080 | tf_op jit(solution)/shard_map/all_gather | solution.py:42
  326.4 193.0 %reduce-scatter.29.cloned.1.call-start = ((), (), s32[]{:S(2)}) async-start(), calls=%async_computation.25 | async-start | bytes 3932160 | tf_op jit(solution)/shard_map/reduce_scatter | solution.py:46
  482.0 64.9 %all-gather.31.cloned.1.call-start = ((), (), s32[]{:S(2)}) async-start(), calls=%async_computation.26 | async-start | bytes 1966080 | tf_op jit(solution)/shard_map/all_gather | solution.py:42
  522.7 68.7 %all-gather.47.cloned.1.call-start = ((), (), s32[]{:S(2)}) async-start(), calls=%async_computation.49 | async-start | bytes 1327104 | tf_op jit(solution)/shard_map/all_gather | solution.py:37
  523.3 87.6 %all-gather.33.cloned.1.call-start = ((), (), s32[]{:S(2)}) async-start(), calls=%async_computation.28 | async-start | bytes 1966080 | tf_op jit(solution)/shard_map/all_gather | solution.py:50
  526.5 133.2 %reduce-scatter.33.cloned.1.call-start = ((), (), s32[]{:S(2)}) async-start(), calls=%async_computation.29 | async-start | bytes 3932160 | tf_op jit(solution)/shard_map/reduce_scatter | solution.py:54
  621.5 78.4 %reduce-scatter.31.cloned.1.call-start = ((), (), s32[]{:S(2)}) async-start(), calls=%async_computation.27 | async-start | bytes 3932160 | tf_op jit(solution)/shard_map/reduce_scatter | solution.py:46
  627.7 97.2 %all-gather.35.cloned.1.call-start = ((), (), s32[]{:S(2)}) async-start(), calls=%async_computation.30 | async-start | bytes 1966080 | tf_op jit(solution)/shard_map/all_gather | solution.py:50
  705.2 87.7 %reduce-scatter.35.cloned.1.call-start = ((), (), s32[]{:S(2)}) async-start(), calls=%async_computation.31 | async-start | bytes 3932160 | tf_op jit(solution)/shard_map/reduce_scatter | solution.py:54
  755.0 63.8 %all-gather.37.cloned.1.call-start = ((), (), s32[]{:S(2)}) async-start(), calls=%async_computation.32 | async-start | bytes 1966080 | tf_op jit(solution)/shard_map/all_gather | solution.py:50
  799.0 69.6 %reduce-scatter.37.cloned.1.call-start = ((), (), s32[]{:S(2)}) async-start(), calls=%async_computation.33 | async-start | bytes 3932160 | tf_op jit(solution)/shard_map/reduce_scatter | solution.py:54
  830.7 67.6 %all-gather.39.cloned.1.call-start = ((), (), s32[]{:S(2)}) async-start(), calls=%async_computation.34 | async-start | bytes 1966080 | tf_op jit(solution)/shard_map/all_gather | solution.py:50
  874.5 73.2 %reduce-scatter.63.cloned.1.call-start = ((), (), s32[]{:S(2)}) async-start(), calls=%async_computation.51 | async-start | bytes 884736
  877.6 135.4 %reduce-scatter.59.cloned.1.call-start = ((), (), s32[]{:S(2)}) async-start(), calls=%async_computation.45 | async-start | bytes 2654208 | tf_op jit(solution)/shard_map/reduce_scatter | solution.py:64
  883.4 201.1 %reduce-scatter.57.cloned.1.call-start = ((), (), s32[]{:S(2)}) async-start(), calls=%async_computation.44 | async-start | bytes 2654208 | tf_op jit(solution)/shard_map/reduce_scatter | solution.py:64
  888.7 267.5 %reduce-scatter.55.cloned.1.call-start = ((), (), s32[]{:S(2)}) async-start(), calls=%async_computation.43 | async-start | bytes 2654208 | tf_op jit(solution)/shard_map/reduce_scatter | solution.py:63
  893.6 334.3 %reduce-scatter.53.cloned.1.call-start = ((), (), s32[]{:S(2)}) async-start(), calls=%async_computation.42 | async-start | bytes 2654208 | tf_op jit(solution)/shard_map/reduce_scatter | solution.py:63
  898.2 394.7 %reduce-scatter.61.cloned.1.call-start = ((), (), s32[]{:S(2)}) async-start(), calls=%async_computation.50 | async-start | bytes 884736
  901.6 456.5 %reduce-scatter.51.cloned.1.call-start = ((), (), s32[]{:S(2)}) async-start(), calls=%async_computation.41 | async-start | bytes 884736 | tf_op jit(solution)/shard_map/reduce_scatter | solution.py:61
  903.2 519.8 %reduce-scatter.49.cloned.1.call-start = ((), (), s32[]{:S(2)}) async-start(), calls=%async_computation.40 | async-start | bytes 884736 | tf_op jit(solution)/shard_map/reduce_scatter | solution.py:61
  914.8 573.5 %reduce-scatter.47.cloned.1.call-start = ((), (), s32[]{:S(2)}) async-start(), calls=%async_computation.39 | async-start | bytes 884736 | tf_op jit(solution)/shard_map/reduce_scatter | solution.py:60
  916.4 636.7 %reduce-scatter.45.cloned.1.call-start = ((), (), s32[]{:S(2)}) async-start(), calls=%async_computation.38 | async-start | bytes 884736 | tf_op jit(solution)/shard_map/reduce_scatter | solution.py:60
  934.0 684.2 %reduce-scatter.43.cloned.1.call-start = ((), (), s32[]{:S(2)}) async-start(), calls=%async_computation.37 | async-start | bytes 884736 | tf_op jit(solution)/shard_map/reduce_scatter | solution.py:59
  936.6 746.4 %reduce-scatter.41.cloned.1.call-start = ((), (), s32[]{:S(2)}) async-start(), calls=%async_computation.36 | async-start | bytes 884736 | tf_op jit(solution)/shard_map/reduce_scatter | solution.py:59
  942.8 779.9 %reduce-scatter.39.cloned.1.call-start = ((), (), s32[]{:S(2)}) async-start(), calls=%async_computation.35 | async-start | bytes 3932160 | tf_op jit(solution)/shard_map/reduce_scatter | solution.py:54
  946.6 897.3 %all-reduce.3.cloned.1.call-start = ((), (), s32[]{:S(2)}) async-start(), calls=%async_computation.52 | async-start | bytes 147456 | tf_op jit(solution)/shard_map/psum | solution.py:332
  (110 other events, 8245.9 us)
Sparse Core Ops, SparseCore 0:
  15.0 22.3 all-gather.24
  171.2 38.8 reduce-scatter.24
  326.6 19.6 all-gather.28
  481.4 38.0 reduce-scatter.28
  621.7 37.9 reduce-scatter.32
  662.0 37.9 reduce-scatter.30
  799.1 19.6 all-gather.36
  874.6 19.6 all-gather.38
  1725.2 118.6 all-reduce.2
Sparse Core Ops, SparseCore 1:
  174.6 42.4 all-gather.40
  219.1 17.9 all-gather.26
  239.9 41.5 all-gather.42
  287.5 36.3 reduce-scatter.26
  485.0 41.6 all-gather.44
  528.9 17.9 all-gather.30
  549.8 41.5 all-gather.46
  592.8 18.0 all-gather.32
  705.3 19.5 all-gather.34
  755.1 37.8 reduce-scatter.34
  830.8 37.8 reduce-scatter.36
  878.9 62.6 reduce-scatter.62
  944.9 68.1 reduce-scatter.58
  1016.5 67.9 reduce-scatter.56
  1088.0 68.1 reduce-scatter.54
  1159.7 68.1 reduce-scatter.52
  1231.2 61.7 reduce-scatter.60
  1296.6 61.5 reduce-scatter.50
  1361.4 61.6 reduce-scatter.48
  1426.7 61.5 reduce-scatter.46
  1491.5 61.6 reduce-scatter.44
  1556.6 61.5 reduce-scatter.42
  1621.4 61.6 reduce-scatter.40
  1685.8 36.8 reduce-scatter.38
where the time goes:
time: 1870 us; the launch traced here: 1860 us
  waiting for transfers between devices  1320 us (71%)
  blocking collectives  252 us (13%)
  matrix products  175 us (9%)
  other arithmetic  62.2 us (3%)
  local copies, waits for them, and re-layouts  29.7 us (2%)
    reduce_scatter x4, waiting for transfers between devices, collect(): lax.psum_scatter(partial_rows, 'tensor', scatter_dimension=0, tiled=True)  147 us
    reduce_scatter x4, waiting for transfers between devices, collect_grad(): lax.psum_scatter(partial_rows, 'tensor', scatter_dimension=0, tiled=True)  146 us
    reduce_scatter x2, waiting for transfers between devices, sum_weights(): lax.psum_scatter(grads[4], 'fsdp', scatter_dimension=0, tiled=True)  141 us
    reduce_scatter x2, waiting for transfers between devices, sum_weights(): lax.psum_scatter(grads[5], 'fsdp', scatter_dimension=1, tiled=True)  135 us
    reduce_scatter x2, waiting for transfers between devices, sum_weights(): lax.psum_scatter(grads[1], 'fsdp', scatter_dimension=0, tiled=True)  128 us
    reduce_scatter x2, waiting for transfers between devices, sum_weights(): lax.psum_scatter(grads[2], 'fsdp', scatter_dimension=0, tiled=True)  128 us
    reduce_scatter x2, waiting for transfers between devices, sum_weights(): lax.psum_scatter(grads[0], 'fsdp', scatter_dimension=0, tiled=True)  128 us
    psum x1, waiting for transfers between devices, local(): lax.psum((jnp.stack(vector_rows), jnp.stack(up_rows)), ('fsdp', 'tensor'))  117 us
  transfers between devices with their start and end apart: 33, of which 28 were waited for; matrix products, arithmetic and copies ran while one was open for 7% of the time, Pallas kernels for 0%

commit v1 on v0

v1 whole, which is shorter than its diff:
```python
import functools

import jax
import jax.numpy as jnp
from jax import lax
from jax.experimental import pallas as pl
from jax.experimental.pallas import tpu as pltpu
from jax.sharding import PartitionSpec as P

HEAD_DIM = 64
EPSILON = 1e-05
LOW = jnp.bfloat16
WIDE = jnp.float32
ROOT = 0.7978845608028654
CUBE = 0.044715

SWAP_CORE = [(0, 1), (1, 0), (2, 3), (3, 2)]
SWAP_Y = [(0, 2), (2, 0), (1, 3), (3, 1)]


def swap_core(value):
    return lax.ppermute(value, "tensor", SWAP_CORE)


def swap_y(value):
    return lax.ppermute(value, "tensor", SWAP_Y)


def dot(a, b):
    return jnp.dot(a, b, preferred_element_type=WIDE)


def dot_nt(a, b):
    return lax.dot_general(a, b, (((1,), (1,)), ((), ())), preferred_element_type=WIDE)


def dot_tn(a, b):
    return lax.dot_general(a, b, (((0,), (0,)), ((), ())), preferred_element_type=WIDE)


def ring_order(count):
    return list(range(0, count, 2)) + list(range(count - 1, 0, -2))


def ring_pairs(count):
    order = ring_order(count)
    pairs = []
    for place, here in enumerate(order):
        for t in range(4):
            step = 1 if t % 2 == 0 else -1
            there = order[(place + step) % count]
            pairs.append((here * 4 + t, there * 4 + t))
    return pairs


def ring_step(value, count):
    return lax.ppermute(value, ("fsdp", "tensor"), ring_pairs(count))


class Ring:
    def __init__(self):
        self.count = lax.axis_size("fsdp")
        self.use = self.count == 8
        if self.use:
            order = ring_order(self.count)
            place = [0] * self.count
            for index, here in enumerate(order):
                place[here] = index
            self.order = jnp.array(order, jnp.int32)
            self.place = jnp.array(place, jnp.int32)[lax.axis_index("fsdp")]
            self.core = lax.axis_index("tensor") % 2
            self.way = 1 - 2 * self.core

    def block_at(self, steps):
        return self.order[(self.place + steps + 2 * self.count) % self.count]

    def gather(self, piece):
        count = self.count
        if not self.use:
            return lax.all_gather(piece, "fsdp", axis=0, tiled=True)
        rows, columns = piece.shape
        half = rows // 2
        whole = jnp.zeros((count * rows, columns), piece.dtype)

        def put(whole, value, block, offset=0):
            return lax.dynamic_update_slice(whole, value, (block * rows + offset, 0))

        whole = put(whole, piece, lax.axis_index("fsdp"))
        current = piece
        for step in range(1, count // 2):
            current = ring_step(current, count)
            whole = put(whole, current, self.block_at(-self.way * step))
            whole = put(whole, swap_core(current), self.block_at(self.way * step))
        last = lax.dynamic_slice(current, (self.core * half, 0), (half, columns))
        last = ring_step(last, count)
        block = self.block_at(count // 2)
        whole = put(whole, last, block, self.core * half)
        whole = put(whole, swap_core(last), block, (1 - self.core) * half)
        return whole

    def scatter(self, partial, own_columns, peer_columns):
        count = self.count
        if not self.use:
            mine = own_columns(partial).astype(WIDE) + swap_core(peer_columns(partial)).astype(WIDE)
            return lax.psum_scatter(mine, "fsdp", scatter_dimension=0, tiled=True)
        rows = partial.shape[0] // count
        columns = partial.shape[1]
        half = rows // 2

        def block(steps, offset=0, size=rows):
            return lax.dynamic_slice(
                partial, (self.block_at(steps) * rows + offset, 0), (size, columns)
            )

        far = count // 2
        give = [block(-self.way * step) for step in range(1, far)]
        give.append(block(far, (1 - self.core) * half, half))
        got = swap_core(jnp.concatenate(give))
        keep = [
            block(self.way * step).astype(WIDE) + got[(step - 1) * rows : step * rows].astype(WIDE)
            for step in range(1, far)
        ]
        last = block(far, self.core * half, half).astype(WIDE) + got[(far - 1) * rows :].astype(WIDE)
        moving = ring_step(last.astype(LOW), count).astype(WIDE)
        blank = jnp.zeros_like(moving)
        moving = jnp.where(
            self.core == 0, jnp.concatenate([moving, blank]), jnp.concatenate([blank, moving])
        )
        for step in range(far - 1, 0, -1):
            moving = ring_step((keep[step - 1] + moving).astype(LOW), count).astype(WIDE)
        total = moving + block(0).astype(WIDE)
        return own_columns(total) + swap_core(peer_columns(total).astype(LOW)).astype(WIDE)


def sum_everywhere(value):
    count = lax.axis_size("fsdp")
    if count & (count - 1):
        return lax.psum(value, ("fsdp", "tensor"))
    value = value + swap_core(value)
    value = value + swap_y(value)
    bit = 1
    while bit < count:
        value = value + lax.ppermute(value, "fsdp", [(i, i ^ bit) for i in range(count)])
        bit *= 2
    return value


SUB = 128


def pair_parts(heads):
    return [(pair, part) for pair in range(heads // 2) for part in range(2)]


def attention_forward_kernel(*refs, heads):
    segq, segk, q_ref = refs[:3]
    k_refs = refs[3:7]
    v_refs = refs[7:11]
    mixed_ref, norm_ref = refs[11:]
    scale = HEAD_DIM ** (-0.5)
    same = segq[...] == segk[...]
    lane = lax.broadcasted_iota(jnp.int32, (1, 128), 1)
    side = [lane < 64, lane >= 64]
    norms = jnp.zeros((SUB, 128), WIDE)
    for pair in range(heads // 2):
        columns = slice(pair * 128, pair * 128 + 128)
        q = q_ref[:, columns]
        total = jnp.zeros((SUB, 128), WIDE)
        for part in range(2):
            q_one = jnp.where(side[part], q, jnp.zeros_like(q))
            scores = jnp.concatenate([dot_nt(q_one, k[:, columns]) for k in k_refs], axis=1)
            scores = jnp.where(same, scores * scale, -jnp.inf)
            top = jnp.max(scores, axis=1, keepdims=True)
            grown = jnp.exp(scores - top)
            bulk = jnp.sum(grown, axis=1, keepdims=True)
            probs = (grown * (1.0 / bulk)).astype(LOW)
            for index, v in enumerate(v_refs):
                block = v[:, columns]
                v_one = jnp.where(side[part], block, jnp.zeros_like(block))
                width = block.shape[0]
                total += dot(probs[:, index * width : (index + 1) * width], v_one)
            norms = jnp.where(lane == pair * 2 + part, top + jnp.log(bulk), norms)
        mixed_ref[:, columns] = total.astype(LOW)
    norm_ref[...] = norms


def attention_forward(segq, segk, q, keys, values):
    rows, width = q.shape
    heads = width // HEAD_DIM
    full = [pl.BlockSpec(k.shape, lambda i: (0, 0)) for k in keys]
    flops = 4 * rows * 4 * rows * width
    return pl.pallas_call(
        functools.partial(attention_forward_kernel, heads=heads),
        grid=(rows // SUB,),
        in_specs=[
            pl.BlockSpec((SUB, 1), lambda i: (i, 0)),
            pl.BlockSpec(segk.shape, lambda i: (0, 0)),
            pl.BlockSpec((SUB, width), lambda i: (i, 0)),
            *full,
            *full,
        ],
        out_specs=[
            pl.BlockSpec((SUB, width), lambda i: (i, 0)),
            pl.BlockSpec((SUB, 128), lambda i: (i, 0)),
        ],
        out_shape=[
            jax.ShapeDtypeStruct((rows, width), LOW),
            jax.ShapeDtypeStruct((rows, 128), WIDE),
        ],
        compiler_params=pltpu.CompilerParams(vmem_limit_bytes=48 << 20),
        cost_estimate=pl.CostEstimate(
            flops=flops, bytes_accessed=10 * rows * width * 2, transcendentals=4 * rows * rows * heads
        ),
    )(segq, segk, q, *keys, *values)


def attention_backward_kernel(*refs, heads, first):
    segq, segk, q_ref, norm_ref, g_ref = refs[:5]
    k_refs = refs[5:9]
    v_refs = refs[9:13]
    if first:
        dq_ref, dk_ref, dv_ref = refs[13:]
    else:
        dk_in, dv_in, dq_ref, dk_ref, dv_ref = refs[13:]
    scale = HEAD_DIM ** (-0.5)

    @pl.when(pl.program_id(0) == 0)
    def _():
        if first:
            dk_ref[...] = jnp.zeros_like(dk_ref)
            dv_ref[...] = jnp.zeros_like(dv_ref)
        else:
            dk_ref[...] = dk_in[...]
            dv_ref[...] = dv_in[...]

    same = segq[...] == segk[...]
    lane = lax.broadcasted_iota(jnp.int32, (1, 128), 1)
    side = [lane < 64, lane >= 64]
    norms = norm_ref[...]
    width = k_refs[0].shape[0]
    for pair in range(heads // 2):
        columns = slice(pair * 128, pair * 128 + 128)
        q = q_ref[:, columns]
        g = g_ref[:, columns]
        dq = jnp.zeros((SUB, 128), WIDE)
        for part in range(2):
            q_one = jnp.where(side[part], q, jnp.zeros_like(q))
            g_one = jnp.where(side[part], g, jnp.zeros_like(g))
            norm = jnp.sum(jnp.where(lane == pair * 2 + part, norms, 0.0), axis=1, keepdims=True)
            scores = jnp.concatenate([dot_nt(q_one, k[:, columns]) for k in k_refs], axis=1)
            probs = jnp.where(same, jnp.exp(scores * scale - norm), 0.0)
            g_probs = jnp.concatenate([dot_nt(g_one, v[:, columns]) for v in v_refs], axis=1)
            row_total = jnp.sum(probs * g_probs, axis=1, keepdims=True)
            g_scores = (probs * (g_probs - row_total)).astype(LOW)
            probs_low = probs.astype(LOW)
            dk_ref[:, columns] += dot_tn(g_scores, q_one)
            dv_ref[:, columns] += dot_tn(probs_low, g_one)
            for index, k in enumerate(k_refs):
                block = k[:, columns]
                k_one = jnp.where(side[part], block, jnp.zeros_like(block))
                dq += dot(g_scores[:, index * width : (index + 1) * width], k_one)
        dq_ref[:, columns] = (dq * scale).astype(LOW)


def attention_backward(segq, segk, q, norms, g, keys, values, sums):
    rows, width = q.shape
    heads = width // HEAD_DIM
    full = [pl.BlockSpec(k.shape, lambda i: (0, 0)) for k in keys]
    length = 4 * keys[0].shape[0]
    whole = pl.BlockSpec((length, width), lambda i: (0, 0))
    first = sums is None
    extra = () if first else tuple(sums)
    return pl.pallas_call(
        functools.partial(attention_backward_kernel, heads=heads, first=first),
        grid=(rows // SUB,),
        in_specs=[
            pl.BlockSpec((SUB, 1), lambda i: (i, 0)),
            pl.BlockSpec(segk.shape, lambda i: (0, 0)),
            pl.BlockSpec((SUB, width), lambda i: (i, 0)),
            pl.BlockSpec((SUB, 128), lambda i: (i, 0)),
            pl.BlockSpec((SUB, width), lambda i: (i, 0)),
            *full,
            *full,
            *([whole] * len(extra)),
        ],
        out_specs=[pl.BlockSpec((SUB, width), lambda i: (i, 0)), whole, whole],
        out_shape=[
            jax.ShapeDtypeStruct((rows, width), LOW),
            jax.ShapeDtypeStruct((length, width), WIDE),
            jax.ShapeDtypeStruct((length, width), WIDE),
        ],
        compiler_params=pltpu.CompilerParams(vmem_limit_bytes=48 << 20),
        cost_estimate=pl.CostEstimate(
            flops=10 * rows * length * width,
            bytes_accessed=10 * rows * width * 2,
            transcendentals=rows * length * heads,
        ),
    )(segq, segk, q, norms, g, *keys, *values, *extra)


def norm_forward(rows, gain, shift):
    center = rows - jnp.mean(rows, axis=1, keepdims=True)
    factor = lax.rsqrt(jnp.mean(center * center, axis=1, keepdims=True) + EPSILON)
    return (center * factor * gain + shift).astype(LOW), factor


def norm_backward(grad, rows, factor, gain):
    normed = (rows - jnp.mean(rows, axis=1, keepdims=True)) * factor
    scaled = grad * gain
    through = factor * (
        scaled
        - jnp.mean(scaled, axis=1, keepdims=True)
        - normed * jnp.mean(scaled * normed, axis=1, keepdims=True)
    )
    return jnp.sum(grad * normed, axis=0), jnp.sum(grad, axis=0), through


def gelu_both(pre):
    inner = jnp.tanh(ROOT * (pre + CUBE * pre * pre * pre))
    slope = 0.5 * (1.0 + inner) + 0.5 * pre * (1.0 - inner * inner) * (
        ROOT * (1.0 + 3.0 * CUBE * pre * pre)
    )
    return (0.5 * pre * (1.0 + inner)).astype(LOW), slope.astype(LOW)


def local(
    hidden_in,
    time_embed,
    segment_ids,
    cotangent,
    query_weight,
    key_weight,
    value_weight,
    output_weight,
    up_weight,
    down_weight,
    query_bias,
    value_bias,
    output_bias,
    up_bias,
    down_bias,
    first_gain,
    first_shift,
    second_gain,
    second_shift,
):
    rows = hidden_in.shape[0]
    layers, _, head_width = query_weight.shape
    hidden_width = up_weight.shape[2]
    place = lax.axis_index("tensor")
    core = place % 2
    side = place // 2
    ring = Ring()

    def low_high(own):
        peer = swap_core(own)
        return jnp.where(core == 0, own, peer), jnp.where(core == 0, peer, own)

    def join(low, high, widths):
        parts, start = [], 0
        for width in widths:
            parts += [low[:, start : start + width], high[:, start : start + width]]
            start += width
        return jnp.concatenate(parts, axis=1)

    widths_a = (head_width,) * 3
    widths_b = (head_width, hidden_width, hidden_width)
    pieces_a, pieces_b = [], []
    packed = [
        jnp.concatenate(
            [
                query_weight[layer],
                key_weight[layer],
                value_weight[layer],
                output_weight[layer].T,
                up_weight[layer],
                down_weight[layer].T,
            ],
            axis=1,
        )
        for layer in range(layers)
    ]
    cut = 3 * head_width
    for layer in range(layers):
        low, high = low_high(packed[layer])
        pieces_a.append(join(low[:, :cut], high[:, :cut], widths_a))
        pieces_b.append(join(low[:, cut:], high[:, cut:], widths_b))

    bias_low, bias_high = low_high(jnp.concatenate([query_bias, value_bias, up_bias], axis=1))
    q_bias = jnp.concatenate([bias_low[:, :head_width], bias_high[:, :head_width]], axis=1)
    v_bias = jnp.concatenate(
        [bias_low[:, head_width : 2 * head_width], bias_high[:, head_width : 2 * head_width]], axis=1
    )
    u_bias = jnp.concatenate([bias_low[:, 2 * head_width :], bias_high[:, 2 * head_width :]], axis=1)

    def both_sides(own):
        other = swap_y(own)
        return [jnp.where(side == 0, own, other), jnp.where(side == 0, other, own)]

    def own_of(pair):
        return jnp.where(side == 0, pair[0], pair[1])

    def other_of(pair):
        return jnp.where(side == 0, pair[1], pair[0])

    segments = segment_ids[0]

    def ids_at(block):
        return lax.dynamic_slice_in_dim(segments, block * rows, rows)

    ids = [ids_at(core), ids_at(2 + core), ids_at(1 - core), ids_at(3 - core)]
    segk = jnp.concatenate(ids)[None, :]
    segq = [ids[0][:, None], ids[1][:, None]]
    own_ids = ids_at(place)
    embed = time_embed.astype(WIDE)

    state = [part.astype(WIDE) + embed for part in both_sides(hidden_in)]
    weights_a = [None] * layers
    weights_b = [None] * layers
    weights_a[0] = ring.gather(pieces_a[0])

    valid = (own_ids >= 0)[:, None]
    seed = jnp.where(valid, cotangent, jnp.zeros_like(cotangent))

    width = 2 * head_width
    hidden = 2 * hidden_width
    kept = []
    denoised = None
    for layer in range(layers):
        w_qkv = weights_a[layer]
        firsts, f_factors, queries, keys, values = [], [], [], [], []
        for j in range(2):
            first, factor = norm_forward(state[j], first_gain[layer], first_shift[layer])
            qkv = dot(first, w_qkv)
            firsts.append(first)
            f_factors.append(factor)
            queries.append((qkv[:, :width] + q_bias[layer]).astype(LOW))
            keys.append(qkv[:, width : 2 * width].astype(LOW))
            values.append((qkv[:, 2 * width :] + v_bias[layer]).astype(LOW))
        if layer == 0:
            weights_b[0] = ring.gather(pieces_b[0])
            weights_a[1] = ring.gather(pieces_a[1])
            weights_b[1] = ring.gather(pieces_b[1])
            seeds = both_sides(seed)
        w_out = weights_b[layer][:, :width]
        w_up = weights_b[layer][:, width : width + hidden]
        w_down = weights_b[layer][:, width + hidden :]
        far = swap_core((keys, values))
        keys = keys + list(far[0])
        values = values + list(far[1])
        mixeds, norms, parts = [], [], []
        for j in range(2):
            mixed, norm = attention_forward(segq[j], segk, queries[j], keys, values)
            mixeds.append(mixed)
            norms.append(norm)
            parts.append(dot_nt(mixed, w_out))
        arrived = [swap_y(part.astype(LOW)) for part in parts]
        middles, seconds, s_factors, acts, slopes, branches = [], [], [], [], [], []
        for j in range(2):
            middle = state[j] + (parts[j] + arrived[j].astype(WIDE)) + output_bias[layer]
            second, factor = norm_forward(middle, second_gain[layer], second_shift[layer])
            act, slope = gelu_both(dot(second, w_up) + u_bias[layer])
            middles.append(middle)
            seconds.append(second)
            s_factors.append(factor)
            acts.append(act)
            slopes.append(slope)
            branches.append(dot_nt(act, w_down))
        if layer < layers - 1:
            arrived = [swap_y(part.astype(LOW)) for part in branches]
            following = [
                middles[j] + (branches[j] + arrived[j].astype(WIDE)) + down_bias[layer]
                for j in range(2)
            ]
        else:
            arrived = swap_y(other_of(branches).astype(LOW))
            denoised = (
                own_of(middles) + own_of(branches) + arrived.astype(WIDE) + down_bias[layer]
            ).astype(LOW)
            following = None
        kept.append(
            (state, firsts, f_factors, queries, keys, values, norms, mixeds, middles, seconds, s_factors, acts, slopes)
        )
        state = following

    grads = [part.astype(WIDE) for part in seeds]
    lows = seeds
    matrix_out = [None] * layers
    vector_rows = []
    input_grad = None

    def wide_at(vector, count):
        spread = jnp.zeros((2 * vector.shape[0],), WIDE)
        return lax.dynamic_update_slice_in_dim(spread, vector, side * vector.shape[0], 0)

    for layer in reversed(range(layers)):
        (state, firsts, f_factors, queries, keys, values, norms, mixeds, middles, seconds, s_factors, acts, slopes) = kept[layer]
        w_qkv = weights_a[layer]
        w_out = weights_b[layer][:, :width]
        w_up = weights_b[layer][:, width : width + hidden]
        w_down = weights_b[layer][:, width + hidden :]
        down_b_grad = jnp.sum(own_of(grads), axis=0)
        g_pres, parts = [], []
        for j in range(2):
            g_pre = (dot(lows[j], w_down) * slopes[j].astype(WIDE)).astype(LOW)
            g_pres.append(g_pre)
            parts.append(dot_nt(g_pre, w_up))
        arrived = [swap_y(part.astype(LOW)) for part in parts]
        rows_of = jnp.concatenate
        d_down = dot_tn(rows_of(lows), rows_of(acts)).astype(LOW)
        d_up = dot_tn(rows_of(seconds), rows_of(g_pres)).astype(LOW)
        up_b_grad = jnp.sum(rows_of(g_pres).astype(WIDE), axis=0)
        g_middles, m_lows, gains, shifts = [], [], [], []
        for j in range(2):
            g_second = parts[j] + arrived[j].astype(WIDE)
            gain, shift, through = norm_backward(
                g_second, middles[j], s_factors[j], second_gain[layer]
            )
            g_middle = grads[j] + through
            g_middles.append(g_middle)
            m_lows.append(g_middle.astype(LOW))
            gains.append(gain)
            shifts.append(shift)
        gain_two, shift_two = own_of(gains), own_of(shifts)
        out_b_grad = jnp.sum(own_of(g_middles), axis=0)
        sums = None
        g_queries = []
        for j in range(2):
            g_mixed = dot(m_lows[j], w_out).astype(LOW)
            g_query, *sums = attention_backward(
                segq[j], segk, queries[j], norms[j], g_mixed, keys, values, sums
            )
            g_queries.append(g_query)
        d_out = dot_tn(rows_of(m_lows), rows_of(mixeds)).astype(LOW)
        near = 2 * rows
        scale = HEAD_DIM ** (-0.5)
        away = swap_core([total[near:].astype(LOW) for total in sums])
        g_key = ((sums[0][:near] + away[0].astype(WIDE)) * scale).astype(LOW)
        g_value = (sums[1][:near] + away[1].astype(WIDE)).astype(LOW)
        g_query = rows_of(g_queries)
        g_qkv = jnp.concatenate([g_query, g_key, g_value], axis=1)
        parts = [dot_nt(g_qkv[:rows], w_qkv), dot_nt(g_qkv[rows:], w_qkv)]
        d_qkv = dot_tn(rows_of(firsts), g_qkv).astype(LOW)
        q_b_grad = jnp.sum(g_query.astype(WIDE), axis=0)
        v_b_grad = jnp.sum(g_value.astype(WIDE), axis=0)
        if layer > 0:
            arrived = [swap_y(part.astype(LOW)) for part in parts]
            gains, shifts, grads, lows = [], [], [], []
            for j in range(2):
                g_first = parts[j] + arrived[j].astype(WIDE)
                gain, shift, through = norm_backward(
                    g_first, state[j], f_factors[j], first_gain[layer]
                )
                grad = g_middles[j] + through
                grads.append(grad)
                lows.append(grad.astype(LOW))
                gains.append(gain)
                shifts.append(shift)
            gain_one, shift_one = own_of(gains), own_of(shifts)
        else:
            arrived = swap_y(other_of(parts).astype(LOW))
            g_first = own_of(parts) + arrived.astype(WIDE)
            gain_one, shift_one, through = norm_backward(
                g_first, own_of(state), own_of(f_factors), first_gain[layer]
            )
            input_grad = own_of(g_middles) + through

        def columns_of(widths, which):
            def pick(array):
                low, high, start = [], [], 0
                for w in widths:
                    low.append(array[:, start : start + w])
                    high.append(array[:, start + w : start + 2 * w])
                    start += 2 * w
                low, high = jnp.concatenate(low, axis=1), jnp.concatenate(high, axis=1)
                return jnp.where(core == which, low, high)

            return pick

        groups = [
            ((hidden_width, hidden_width), jnp.concatenate([d_up, d_down], axis=1)),
            ((head_width,) * 4, jnp.concatenate([d_qkv, d_out], axis=1)),
        ]
        done = [
            ring.scatter(array, columns_of(widths, 0), columns_of(widths, 1))
            for widths, array in groups
        ]
        heads_of = lambda i: done[1][:, i * head_width : (i + 1) * head_width]
        matrix_out[layer] = (
            heads_of(0),
            heads_of(1),
            heads_of(2),
            heads_of(3).T,
            done[0][:, :hidden_width],
            done[0][:, hidden_width:].T,
        )
        vector_rows = [
            jnp.concatenate(
                [
                    jnp.stack(
                        [
                            gain_one,
                            shift_one,
                            gain_two,
                            shift_two,
                            out_b_grad,
                            down_b_grad,
                            wide_at(q_b_grad, 0),
                            wide_at(v_b_grad, 0),
                        ]
                    ).reshape(-1),
                    wide_at(up_b_grad, 0),
                ]
            )
        ] + vector_rows
    depth = hidden_in.shape[1]
    total = sum_everywhere(jnp.stack(vector_rows).reshape(-1, 128)).reshape(layers, -1)
    vectors = total[:, : 8 * depth].reshape(layers, 8, depth)
    ups = total[:, 8 * depth :]
    stacked = [jnp.stack([matrix_out[layer][index] for layer in range(layers)]) for index in range(6)]

    def mine(array, size):
        return lax.dynamic_slice_in_dim(array, place * size, size, 1)

    return (
        denoised,
        input_grad,
        *stacked,
        mine(vectors[:, 6], head_width),
        mine(vectors[:, 7], head_width),
        vectors[:, 4],
        mine(ups, hidden_width),
        vectors[:, 5],
        vectors[:, 0],
        vectors[:, 1],
        vectors[:, 2],
        vectors[:, 3],
    )


def solution(mesh):
    rows = P(("fsdp", "tensor"), None)
    inner = P(None, "fsdp", "tensor")
    outer = P(None, "tensor", "fsdp")
    cut = P(None, "tensor")
    in_specs = (
        rows,
        P("fsdp", None),
        P("fsdp", None),
        rows,
        inner,
        inner,
        inner,
        outer,
        inner,
        outer,
        cut,
        cut,
        P(),
        cut,
        P(),
        P(),
        P(),
        P(),
        P(),
    )
    out_specs = (
        rows,
        rows,
        inner,
        inner,
        inner,
        outer,
        inner,
        outer,
        cut,
        cut,
        P(),
        cut,
        P(),
        P(),
        P(),
        P(),
        P(),
    )
    return jax.shard_map(local, mesh=mesh, in_specs=in_specs, out_specs=out_specs, check_vma=False)
```

time: 1870 us -> 518 us (0.28)
  waiting for transfers between devices: 1320 us -> 180 us
  blocking collectives: 252 us -> 0 us
  matrix products: 175 us -> 46.7 us
  Pallas kernels: 0 us -> 59.1 us
  starting transfers between devices: 2.85 us -> 57.2 us
  local copies, waits for them, and re-layouts: 29.7 us -> 74.3 us
    reduce_scatter x18 -> x0, waiting for transfers between devices: 954 us -> none  [the longest x4 147 us: collect(): lax.psum_scatter(partial_rows, 'tensor', scatter_dimension=0, tiled=True)]
    all_gather x8 -> x0, blocking collectives: 252 us -> none  [the longest x2 66.1 us: fetch(): lax.all_gather(pieces[3], 'fsdp', axis=1, tiled=True)]
    all_gather x12 -> x0, waiting for transfers between devices: 181 us -> none  [the longest x2 79.1 us: fetch(): lax.all_gather(pieces[5], 'fsdp', axis=1, tiled=True)]
    ppermute x0 -> x92, waiting for transfers between devices: none -> 180 us  [the longest x17 90.9 us: swap_y(): return lax.ppermute(value, 'tensor', SWAP_Y)]
    psum x1 -> x0, waiting for transfers between devices: 117 us -> none  [local(): lax.psum((jnp.stack(vector_rows), jnp.stack(up_rows)), ('fsdp', 'tensor'))]
    dot_general x44 -> x40, matrix products: 149 us -> 46.7 us  [the longest x16 20.2 us: dot(): return jnp.dot(a, b, preferred_element_type=WIDE)]
    unnamed x35 -> x0, waiting for transfers between devices: 64.4 us -> none
    pallas_call x0 -> x8, Pallas kernels: none -> 59.1 us  [the longest x4 35.8 us: attention_backward(): pl.pallas_call(functools.partial(attention_backward_kernel, heads=heads,...]
  transfers between devices with their start and end apart: 33 -> 92, of which waited for: 28 -> 43; matrix products, arithmetic and copies ran while one was open for 7% -> 30% of each run, Pallas kernels for 0% -> 12%
where the time goes in v1:
time: 518 us; the launch traced here: 510 us
  waiting for transfers between devices  180 us (35%)
  other arithmetic  77.6 us (15%)
  local copies, waits for them, and re-layouts  74.3 us (14%)
  Pallas kernels  59.1 us (11%)
  starting transfers between devices  57.2 us (11%)
  matrix products  46.7 us (9%)
  between operations  15.2 us (3%)
    ppermute x17, waiting for transfers between devices, swap_y(): return lax.ppermute(value, 'tensor', SWAP_Y)  90.9 us
    ppermute x32, waiting for transfers between devices, ring_step(): return lax.ppermute(value, ('fsdp', 'tensor'), ring_pairs(count))  74.2 us
    pallas_call x4, Pallas kernels, attention_backward(): pl.pallas_call(functools.partial(attention_backward_kernel, heads=heads,...  35.8 us
    ppermute x32, starting transfers between devices, ring_step(): return lax.ppermute(value, ('fsdp', 'tensor'), ring_pairs(count))  29.4 us
    unnamed x337, local copies, waits for them, and re-layouts  23.3 us
    pallas_call x4, Pallas kernels, attention_forward(): pl.pallas_call(functools.partial(attention_forward_kernel, heads=heads),...  23.3 us
    dot_general x16, matrix products, dot(): return jnp.dot(a, b, preferred_element_type=WIDE)  20.2 us
    ppermute x17, starting transfers between devices, swap_y(): return lax.ppermute(value, 'tensor', SWAP_Y)  19.8 us
  transfers between devices with their start and end apart: 92, of which 43 were waited for; matrix products, arithmetic and copies ran while one was open for 30% of the time, Pallas kernels for 12%

profile of v1, /device:TPU:0, one launch (start us, length us, event | category | flops | bytes accessed | tf_op | source)
XLA Modules:
  0.0 510.1 jit_solution(1565493615627941441)
XLA Ops:
  60.4 4.5 collective-permute-done.28
  72.5 4.4 collective-permute-done.6
  91.7 5.8 %shard_map.333 = (bf16[256,384]{1,0:T(8,128)(2,1)S(1)}, f32[256,128]{1,0:T(8,128)S(1)}) custom-call(s32[256,1]{1,0:T(8,128)S(1)} %copy.46.refs_0_, s32[1,1024]{1,0:T(1,128)S(1)} %bitcast.133, bf16[256,384]{1,0:T(8,128)(2,1)S(1)} %get-tuple-element.200.refs_2_, bf16[256,384]{1,0:T(8,128)(2,1)S(1)} %slice.1011.refs_3_.refs_5_, ...), custom_call_target="tpu_custom_call" | custom-call | flops 402653184 | bytes 1966080 | tf_op jit(solution)/shard_map/pallas_call | solution.py:192
  98.1 5.8 %shard_map.332 = (bf16[256,384]{1,0:T(8,128)(2,1)S(1)}, f32[256,128]{1,0:T(8,128)S(1)}) custom-call(s32[256,1]{1,0:T(8,128)S(1)} %copy.44.refs_0_, s32[1,1024]{1,0:T(1,128)S(1)} %bitcast.134, bf16[256,384]{1,0:T(8,128)(2,1)S(1)} %get-tuple-element.299.refs_2_, bf16[256,384]{1,0:T(8,128)(2,1)S(1)} %slice.1011.refs_3_.refs_5_, ...), custom_call_target="tpu_custom_call" | custom-call | flops 402653184 | bytes 1966080 | tf_op jit(solution)/shard_map/pallas_call | solution.py:192
  109.5 5.5 %collective-permute-done.19 = bf16[96,3456]{1,0:T(8,128)(2,1)S(1)} collective-permute-done((bf16[96,3456]{1,0:T(8,128)(2,1)S(1)}, bf16[96,3456]{1,0:T(8,128)(2,1)S(1)}, u32[]{:S(2)}, u32[]{:S(2)}) %collective-permute-start.19) | collective-permute-done | bytes 663584 | tf_op jit(solution)/shard_map/ppermute | solution.py:57
  116.2 5.9 %collective-permute-done.44 = bf16[96,3456]{1,0:T(8,128)(2,1)S(1)} collective-permute-done((bf16[96,3456]{1,0:T(8,128)(2,1)S(1)}, bf16[96,3456]{1,0:T(8,128)(2,1)S(1)}, u32[]{:S(2)}, u32[]{:S(2)}) %collective-permute-start.44) | collective-permute-done | bytes 663584 | tf_op jit(solution)/shard_map/ppermute | solution.py:57
  133.6 8.5 %collective-permute-done.34 = bf16[256,768]{1,0:T(8,128)(2,1)S(1)} collective-permute-done((bf16[256,768]{1,0:T(8,128)(2,1)S(1)}, bf16[256,768]{1,0:T(8,128)(2,1)S(1)}, u32[]{:S(2)}, u32[]{:S(2)}) %collective-permute-start.34) | collective-permute-done | bytes 393248 | tf_op jit(solution)/shard_map/ppermute | solution.py:26
  142.1 8.0 %collective-permute-done.23 = bf16[256,768]{1,0:T(8,128)(2,1)S(1)} collective-permute-done((bf16[256,768]{1,0:T(8,128)(2,1)S(1)}, bf16[256,768]{1,0:T(8,128)(2,1)S(1)}, u32[]{:S(2)}, u32[]{:S(2)}) %collective-permute-start.23) | collective-permute-done | bytes 393248 | tf_op jit(solution)/shard_map/ppermute | solution.py:26
  160.6 6.2 %collective-permute-done.35 = bf16[256,768]{1,0:T(8,128)(2,1)S(1)} collective-permute-done((bf16[256,768]{1,0:T(8,128)(2,1)S(1)}, bf16[256,768]{1,0:T(8,128)(2,1)S(1)}, u32[]{:S(2)}, u32[]{:S(2)}) %collective-permute-start.35) | collective-permute-done | bytes 393248 | tf_op jit(solution)/shard_map/ppermute | solution.py:26
  166.8 7.1 %collective-permute-done.24 = bf16[256,768]{1,0:T(8,128)(2,1)S(1)} collective-permute-done((bf16[256,768]{1,0:T(8,128)(2,1)S(1)}, bf16[256,768]{1,0:T(8,128)(2,1)S(1)}, u32[]{:S(2)}, u32[]{:S(2)}) %collective-permute-start.24) | collective-permute-done | bytes 393248 | tf_op jit(solution)/shard_map/ppermute | solution.py:26
  179.2 5.8 %shard_map.335 = (bf16[256,384]{1,0:T(8,128)(2,1)S(1)}, f32[256,128]{1,0:T(8,128)S(1)}) custom-call(s32[256,1]{1,0:T(8,128)S(1)} %copy.46.refs_0_, s32[1,1024]{1,0:T(1,128)S(1)} %bitcast.135, bf16[256,384]{1,0:T(8,128)(2,1)S(1)} %get-tuple-element.196.refs_2_, bf16[256,384]{1,0:T(8,128)(2,1)S(1)} %slice.1009.refs_3_.refs_5_, ...), custom_call_target="tpu_custom_call" | custom-call | flops 402653184 | bytes 1966080 | tf_op jit(solution)/shard_map/pallas_call | solution.py:192
  188.2 6.0 %shard_map.334 = (bf16[256,384]{1,0:T(8,128)(2,1)S(1)}, f32[256,128]{1,0:T(8,128)S(1)}) custom-call(s32[256,1]{1,0:T(8,128)S(1)} %copy-done.23, s32[1,1024]{1,0:T(1,128)S(1)} %bitcast.136, bf16[256,384]{1,0:T(8,128)(2,1)S(1)} %get-tuple-element.301.refs_2_, bf16[256,384]{1,0:T(8,128)(2,1)S(1)} %slice.1009.refs_3_.refs_5_, ...), custom_call_target="tpu_custom_call" | custom-call | flops 402653184 | bytes 1966080 | tf_op jit(solution)/shard_map/pallas_call | solution.py:192
  198.4 7.9 %collective-permute-done.48 = bf16[256,768]{1,0:T(8,128)(2,1)S(1)} collective-permute-done((bf16[256,768]{1,0:T(8,128)(2,1)S(1)}, bf16[256,768]{1,0:T(8,128)(2,1)S(1)}, u32[]{:S(2)}, u32[]{:S(2)}) %collective-permute-start.48) | collective-permute-done | bytes 393248 | tf_op jit(solution)/shard_map/ppermute | solution.py:26
  229.2 4.5 collective-permute-done.52
  233.7 8.4 %collective-permute-done.50 = bf16[256,768]{1,0:T(8,128)(2,1)} collective-permute-done((bf16[256,768]{1,0:T(8,128)(2,1)}, bf16[256,768]{1,0:T(8,128)(2,1)}, u32[]{:S(2)}, u32[]{:S(2)}) %collective-permute-start.50) | collective-permute-done | bytes 393248 | tf_op jit(solution)/shard_map/ppermute | solution.py:26
  242.1 7.0 %collective-permute-done.53 = bf16[256,768]{1,0:T(8,128)(2,1)} collective-permute-done((bf16[256,768]{1,0:T(8,128)(2,1)}, bf16[256,768]{1,0:T(8,128)(2,1)}, u32[]{:S(2)}, u32[]{:S(2)}) %collective-permute-start.53) | collective-permute-done | bytes 393248 | tf_op jit(solution)/shard_map/ppermute | solution.py:26
  249.2 4.2 multiply_reduce_fusion
  258.5 8.0 %shard_map.336 = (bf16[256,384]{1,0:T(8,128)(2,1)S(1)}, f32[1024,384]{1,0:T(8,128)S(1)}, f32[1024,384]{1,0:T(8,128)S(1)}) custom-call(s32[256,1]{1,0:T(8,128)S(1)} %copy-done.24, s32[1,1024]{1,0:T(1,128)S(1)} %bitcast.137, bf16[256,384]{1,0:T(8,128)(2,1)S(1)} %copy-done.9, f32[256,128]{1,0:T(8,128)S(1)} %copy-done.29, ...), custom_call_target="tpu_custom_call" | custom-call | flops 1006632960 | bytes 1966080 | tf_op jit(solution)/shard_map/pallas_call | solution.py:273
  268.9 10.0 %shard_map.337 = (bf16[256,384]{1,0:T(8,128)(2,1)S(1)}, f32[1024,384]{1,0:T(8,128)S(1)}, f32[1024,384]{1,0:T(8,128)S(1)}) custom-call(s32[256,1]{1,0:T(8,128)S(1)} %copy.46.refs_0_, s32[1,1024]{1,0:T(1,128)S(1)} %bitcast.138, bf16[256,384]{1,0:T(8,128)(2,1)S(1)} %get-tuple-element.196.refs_2_, f32[256,128]{1,0:T(8,128)S(1)} %copy-done.21, ...), custom_call_target="tpu_custom_call" | custom-call | flops 1006632960 | bytes 1966080 | tf_op jit(solution)/shard_map/pallas_call | solution.py:273
  288.7 8.7 %collective-permute-done.56 = bf16[256,768]{1,0:T(8,128)(2,1)S(1)} collective-permute-done((bf16[256,768]{1,0:T(8,128)(2,1)S(1)}, bf16[256,768]{1,0:T(8,128)(2,1)S(1)}, u32[]{:S(2)}, u32[]{:S(2)}) %collective-permute-start.56) | collective-permute-done | bytes 393248 | tf_op jit(solution)/shard_map/ppermute | solution.py:26
  297.5 7.6 %collective-permute-done.58 = bf16[256,768]{1,0:T(8,128)(2,1)S(1)} collective-permute-done((bf16[256,768]{1,0:T(8,128)(2,1)S(1)}, bf16[256,768]{1,0:T(8,128)(2,1)S(1)}, u32[]{:S(2)}, u32[]{:S(2)}) %collective-permute-start.58) | collective-permute-done | bytes 393248 | tf_op jit(solution)/shard_map/ppermute | solution.py:26
  326.2 5.8 %collective-permute-done.57 = bf16[256,768]{1,0:T(8,128)(2,1)S(1)} collective-permute-done((bf16[256,768]{1,0:T(8,128)(2,1)}, bf16[256,768]{1,0:T(8,128)(2,1)S(1)}, u32[]{:S(2)}, u32[]{:S(2)}) %collective-permute-start.57) | collective-permute-done | bytes 393248 | tf_op jit(solution)/shard_map/ppermute | solution.py:26
  332.1 6.7 %collective-permute-done.59 = bf16[256,768]{1,0:T(8,128)(2,1)S(1)} collective-permute-done((bf16[256,768]{1,0:T(8,128)(2,1)}, bf16[256,768]{1,0:T(8,128)(2,1)S(1)}, u32[]{:S(2)}, u32[]{:S(2)}) %collective-permute-start.59) | collective-permute-done | bytes 393248 | tf_op jit(solution)/shard_map/ppermute | solution.py:26
  347.1 8.0 %shard_map.338 = (bf16[256,384]{1,0:T(8,128)(2,1)S(1)}, f32[1024,384]{1,0:T(8,128)S(1)}, f32[1024,384]{1,0:T(8,128)S(1)}) custom-call(s32[256,1]{1,0:T(8,128)S(1)} %copy-done.25, s32[1,1024]{1,0:T(1,128)S(1)} %bitcast.139, bf16[256,384]{1,0:T(8,128)(2,1)S(1)} %copy-done.7, f32[256,128]{1,0:T(8,128)S(1)} %copy-done.27, ...), custom_call_target="tpu_custom_call" | custom-call | flops 1006632960 | bytes 1966080 | tf_op jit(solution)/shard_map/pallas_call | solution.py:273
  358.9 9.9 %shard_map.339 = (bf16[256,384]{1,0:T(8,128)(2,1)S(1)}, f32[1024,384]{1,0:T(8,128)S(1)}, f32[1024,384]{1,0:T(8,128)S(1)}) custom-call(s32[256,1]{1,0:T(8,128)S(1)} %copy.46.refs_0_, s32[1,1024]{1,0:T(1,128)S(1)} %bitcast.140, bf16[256,384]{1,0:T(8,128)(2,1)S(1)} %get-tuple-element.200.refs_2_, f32[256,128]{1,0:T(8,128)S(1)} %copy-done.19, ...), custom_call_target="tpu_custom_call" | custom-call | flops 1006632960 | bytes 1966080 | tf_op jit(solution)/shard_map/pallas_call | solution.py:273
  411.1 3.7 collective-permute-done.88
  415.9 5.1 %collective-permute-done.89 = f32[144,128]{1,0:T(8,128)S(1)} collective-permute-done((f32[144,128]{1,0:T(8,128)S(1)}, f32[144,128]{1,0:T(8,128)S(1)}, u32[]{:S(2)}, u32[]{:S(2)}) %collective-permute-start.89) | collective-permute-done | bytes 73760 | tf_op jit(solution)/shard_map/ppermute | solution.py:143
  445.1 9.2 %collective-permute-done.64 = bf16[48,1536]{1,0:T(8,128)(2,1)S(1)} collective-permute-done((bf16[48,1536]{1,0:T(8,128)(2,1)S(1)}, bf16[48,1536]{1,0:T(8,128)(2,1)S(1)}, u32[]{:S(2)}, u32[]{:S(2)}) %collective-permute-start.64) | collective-permute-done | bytes 147488 | tf_op jit(solution)/shard_map/ppermute | solution.py:57
  456.6 5.5 %collective-permute-done.65 = bf16[96,1536]{1,0:T(8,128)(2,1)S(1)} collective-permute-done((bf16[96,1536]{1,0:T(8,128)(2,1)S(1)}, bf16[96,1536]{1,0:T(8,128)(2,1)S(1)}, u32[]{:S(2)}, u32[]{:S(2)}) %collective-permute-start.65) | collective-permute-done | bytes 294944 | tf_op jit(solution)/shard_map/ppermute | solution.py:57
  472.6 7.2 %collective-permute-done.67 = bf16[96,1536]{1,0:T(8,128)(2,1)S(1)} collective-permute-done((bf16[96,1536]{1,0:T(8,128)(2,1)S(1)}, bf16[96,1536]{1,0:T(8,128)(2,1)S(1)}, u32[]{:S(2)}, u32[]{:S(2)}) %collective-permute-start.67) | collective-permute-done | bytes 294944 | tf_op jit(solution)/shard_map/ppermute | solution.py:57
  481.6 4.5 collective-permute-done.85
  487.3 5.1 collective-permute-done.78
  (813 shorter events, 284.4 us)
Async XLA Ops:
  5.7 28.7 %collective-permute-start.25 = (bf16[96,2304]{1,0:T(8,128)(2,1)S(1)}, bf16[96,2304]{1,0:T(8,128)(2,1)S(1)}, u32[]{:S(2)}, u32[]{:S(2)}) collective-permute-start(bf16[96,2304]{1,0:T(8,128)(2,1)S(1)} %concatenate.183), channel_id=1, source_target_pairs={{0,1},{1,0},{2,3},{3,2},{4,5},{5,4},{6,7},{7,6},{8,9},{9,8},{10,11... | collective-permute-start | bytes 1327112 | tf_op jit(solution)/shard_map/ppermute | solution.py:22
  6.5 25.3 %collective-permute-start.1 = (bf16[96,2304]{1,0:T(8,128)(2,1)S(1)}, bf16[96,2304]{1,0:T(8,128)(2,1)}, u32[]{:S(2)}, u32[]{:S(2)}) collective-permute-start(bf16[96,2304]{1,0:T(8,128)(2,1)S(1)} %concatenate.176), channel_id=1, source_target_pairs={{0,1},{1,0},{2,3},{3,2},{4,5},{5,4},{6,7},{7,6},{8,9},{9,8},{10,11... | collective-permute-start | bytes 1327112 | tf_op jit(solution)/shard_map/ppermute | solution.py:22
  6.6 21.0 %collective-permute-start = (bf16[256,768]{1,0:T(8,128)(2,1)S(1)}, bf16[256,768]{1,0:T(8,128)(2,1)S(1)}, u32[]{:S(2)}, u32[]{:S(2)}) collective-permute-start(bf16[256,768]{1,0:T(8,128)(2,1)S(1)} %copy-done.108), channel_id=1, source_target_pairs={{0,2},{2,0},{1,3},{3,1},{4,6},{6,4},{5,7},{7,5},{8,10},{10,8},{9,1... | collective-permute-start | bytes 1179656 | tf_op jit(solution)/shard_map/ppermute | solution.py:26
  9.7 15.8 %collective-permute-start.10 = (f32[2,1152]{1,0:T(2,128)S(1)}, f32[2,1152]{1,0:T(2,128)S(1)}, u32[]{:S(2)}, u32[]{:S(2)}) collective-permute-start(f32[2,1152]{1,0:T(2,128)S(1)} %concatenate.178), channel_id=1, source_target_pairs={{0,1},{1,0},{2,3},{3,2},{4,5},{5,4},{6,7},{7,6},{8,9},{9,8},{10,11... | collective-permute-start | bytes 27656 | tf_op jit(solution)/shard_map/ppermute | solution.py:22
  38.2 17.9 %collective-permute-start.26 = (bf16[96,1152]{1,0:T(8,128)(2,1)}, bf16[96,1152]{1,0:T(8,128)(2,1)}, u32[]{:S(2)}, u32[]{:S(2)}) collective-permute-start(bf16[96,1152]{1,0:T(8,128)(2,1)} %concatenate.184), channel_id=1, source_target_pairs={{0,8},{1,5},{2,10},{3,7},{8,16},{9,1},{10,18},{11,3},{16,24},{17,9... | collective-permute-start | bytes 663560 | tf_op jit(solution)/shard_map/ppermute | solution.py:57
  41.4 15.2 %collective-permute-start.2 = (bf16[96,1152]{1,0:T(8,128)(2,1)}, bf16[96,1152]{1,0:T(8,128)(2,1)}, u32[]{:S(2)}, u32[]{:S(2)}) collective-permute-start(bf16[96,1152]{1,0:T(8,128)(2,1)} %concatenate.177), channel_id=1, source_target_pairs={{0,8},{1,5},{2,10},{3,7},{8,16},{9,1},{10,18},{11,3},{16,24},{17,9... | collective-permute-start | bytes 663560 | tf_op jit(solution)/shard_map/ppermute | solution.py:57
  43.3 36.3 %collective-permute-start.15 = (bf16[96,3456]{1,0:T(8,128)(2,1)S(1)}, bf16[96,3456]{1,0:T(8,128)(2,1)}, u32[]{:S(2)}, u32[]{:S(2)}) collective-permute-start(bf16[96,3456]{1,0:T(8,128)(2,1)S(1)} %concatenate.181), channel_id=1, source_target_pairs={{0,8},{1,5},{2,10},{3,7},{8,16},{9,1},{10,18},{11,3},{16,24},{17,9... | collective-permute-start | bytes 1990664 | tf_op jit(solution)/shard_map/ppermute | solution.py:57
  51.7 29.7 %collective-permute-start.40 = (bf16[96,3456]{1,0:T(8,128)(2,1)}, bf16[96,3456]{1,0:T(8,128)(2,1)S(1)}, u32[]{:S(2)}, u32[]{:S(2)}) collective-permute-start(bf16[96,3456]{1,0:T(8,128)(2,1)} %concatenate.185), channel_id=1, source_target_pairs={{0,8},{1,5},{2,10},{3,7},{8,16},{9,1},{10,18},{11,3},{16,24},{17,9... | collective-permute-start | bytes 1990664 | tf_op jit(solution)/shard_map/ppermute | solution.py:57
  81.3 23.0 %collective-permute-start.16 = (bf16[96,3456]{1,0:T(8,128)(2,1)}, bf16[96,3456]{1,0:T(8,128)(2,1)S(1)}, u32[]{:S(2)}, u32[]{:S(2)}) collective-permute-start(bf16[96,3456]{1,0:T(8,128)(2,1)} %collective-permute-done.15), channel_id=1, source_target_pairs={{0,1},{1,0},{2,3},{3,2},{4,5},{5,4},{6,7},{7,6},{8,9},{9,8},{10,11... | collective-permute-start | bytes 1990664 | tf_op jit(solution)/shard_map/ppermute | solution.py:22
  83.2 20.7 %collective-permute-start.17 = (bf16[96,3456]{1,0:T(8,128)(2,1)}, bf16[96,3456]{1,0:T(8,128)(2,1)S(1)}, u32[]{:S(2)}, u32[]{:S(2)}) collective-permute-start(bf16[96,3456]{1,0:T(8,128)(2,1)} %collective-permute-done.15), channel_id=1, source_target_pairs={{0,8},{1,5},{2,10},{3,7},{8,16},{9,1},{10,18},{11,3},{16,24},{17,9... | collective-permute-start | bytes 1990664 | tf_op jit(solution)/shard_map/ppermute | solution.py:57
  84.4 21.1 %collective-permute-start.42 = (bf16[96,3456]{1,0:T(8,128)(2,1)S(1)}, bf16[96,3456]{1,0:T(8,128)(2,1)S(1)}, u32[]{:S(2)}, u32[]{:S(2)}) collective-permute-start(bf16[96,3456]{1,0:T(8,128)(2,1)S(1)} %collective-permute-done.40), channel_id=1, source_target_pairs={{0,8},{1,5},{2,10},{3,7},{8,16},{9,1},{10,18},{11,3},{16,24},{17,9... | collective-permute-start | bytes 1990664 | tf_op jit(solution)/shard_map/ppermute | solution.py:57
  91.0 104.2 %collective-permute-start.51 = (bf16[256,768]{1,0:T(8,128)(2,1)S(1)}, bf16[256,768]{1,0:T(8,128)(2,1)}, u32[]{:S(2)}, u32[]{:S(2)}) collective-permute-start(bf16[256,768]{1,0:T(8,128)(2,1)S(1)} %copy-done.109), channel_id=1, source_target_pairs={{0,2},{2,0},{1,3},{3,1},{4,6},{6,4},{5,7},{7,5},{8,10},{10,8},{9,1... | collective-permute-start | bytes 1179656 | tf_op jit(solution)/shard_map/ppermute | solution.py:26
  91.5 14.1 %collective-permute-start.41 = (bf16[96,3456]{1,0:T(8,128)(2,1)S(1)}, bf16[96,3456]{1,0:T(8,128)(2,1)}, u32[]{:S(2)}, u32[]{:S(2)}) collective-permute-start(bf16[96,3456]{1,0:T(8,128)(2,1)S(1)} %collective-permute-done.40), channel_id=1, source_target_pairs={{0,1},{1,0},{2,3},{3,2},{4,5},{5,4},{6,7},{7,6},{8,9},{9,8},{10,11... | collective-permute-start | bytes 1990664 | tf_op jit(solution)/shard_map/ppermute | solution.py:22
  103.9 19.6 %collective-permute-start.18 = (bf16[96,3456]{1,0:T(8,128)(2,1)S(1)}, bf16[96,3456]{1,0:T(8,128)(2,1)S(1)}, u32[]{:S(2)}, u32[]{:S(2)}) collective-permute-start(bf16[96,3456]{1,0:T(8,128)(2,1)S(1)} %collective-permute-done.17), channel_id=1, source_target_pairs={{0,1},{1,0},{2,3},{3,2},{4,5},{5,4},{6,7},{7,6},{8,9},{9,8},{10,11... | collective-permute-start | bytes 1990664 | tf_op jit(solution)/shard_map/ppermute | solution.py:22
  105.5 18.2 %collective-permute-start.43 = (bf16[96,3456]{1,0:T(8,128)(2,1)S(1)}, bf16[96,3456]{1,0:T(8,128)(2,1)S(1)}, u32[]{:S(2)}, u32[]{:S(2)}) collective-permute-start(bf16[96,3456]{1,0:T(8,128)(2,1)S(1)} %collective-permute-done.42), channel_id=1, source_target_pairs={{0,1},{1,0},{2,3},{3,2},{4,5},{5,4},{6,7},{7,6},{8,9},{9,8},{10,11... | collective-permute-start | bytes 1990664 | tf_op jit(solution)/shard_map/ppermute | solution.py:22
  105.7 16.5 %collective-permute-start.44 = (bf16[96,3456]{1,0:T(8,128)(2,1)S(1)}, bf16[96,3456]{1,0:T(8,128)(2,1)S(1)}, u32[]{:S(2)}, u32[]{:S(2)}) collective-permute-start(bf16[96,3456]{1,0:T(8,128)(2,1)S(1)} %collective-permute-done.42), channel_id=1, source_target_pairs={{0,8},{1,5},{2,10},{3,7},{8,16},{9,1},{10,18},{11,3},{16,24},{17,9... | collective-permute-start | bytes 1990664 | tf_op jit(solution)/shard_map/ppermute | solution.py:57
  129.5 47.9 %collective-permute-start.47 = (bf16[48,3456]{1,0:T(8,128)(2,1)S(1)}, bf16[48,3456]{1,0:T(8,128)(2,1)S(1)}, u32[]{:S(2)}, u32[]{:S(2)}) collective-permute-start(bf16[48,3456]{1,0:T(8,128)(2,1)S(1)} %collective-permute-done.46), channel_id=1, source_target_pairs={{0,1},{1,0},{2,3},{3,2},{4,5},{5,4},{6,7},{7,6},{8,9},{9,8},{10,11... | collective-permute-start | bytes 995336 | tf_op jit(solution)/shard_map/ppermute | solution.py:22
  132.1 18.0 %collective-permute-start.23 = (bf16[256,768]{1,0:T(8,128)(2,1)S(1)}, bf16[256,768]{1,0:T(8,128)(2,1)S(1)}, u32[]{:S(2)}, u32[]{:S(2)}) collective-permute-start(bf16[256,768]{1,0:T(8,128)(2,1)S(1)} %get-tuple-element.329), channel_id=1, source_target_pairs={{0,2},{2,0},{1,3},{3,1},{4,6},{6,4},{5,7},{7,5},{8,10},{10,8},{9,1... | collective-permute-start | bytes 1179656 | tf_op jit(solution)/shard_map/ppermute | solution.py:26
  159.3 14.6 %collective-permute-start.24 = (bf16[256,768]{1,0:T(8,128)(2,1)S(1)}, bf16[256,768]{1,0:T(8,128)(2,1)S(1)}, u32[]{:S(2)}, u32[]{:S(2)}) collective-permute-start(bf16[256,768]{1,0:T(8,128)(2,1)S(1)} %get-tuple-element.335), channel_id=1, source_target_pairs={{0,2},{2,0},{1,3},{3,1},{4,6},{6,4},{5,7},{7,5},{8,10},{10,8},{9,1... | collective-permute-start | bytes 1179656 | tf_op jit(solution)/shard_map/ppermute | solution.py:26
  224.7 17.4 %collective-permute-start.50 = (bf16[256,768]{1,0:T(8,128)(2,1)}, bf16[256,768]{1,0:T(8,128)(2,1)}, u32[]{:S(2)}, u32[]{:S(2)}) collective-permute-start(bf16[256,768]{1,0:T(8,128)(2,1)} %get-tuple-element.351), channel_id=1, source_target_pairs={{0,2},{2,0},{1,3},{3,1},{4,6},{6,4},{5,7},{7,5},{8,10},{10,8},{9,1... | collective-permute-start | bytes 1179656 | tf_op jit(solution)/shard_map/ppermute | solution.py:26
  225.2 23.9 %collective-permute-start.53 = (bf16[256,768]{1,0:T(8,128)(2,1)}, bf16[256,768]{1,0:T(8,128)(2,1)}, u32[]{:S(2)}, u32[]{:S(2)}) collective-permute-start(bf16[256,768]{1,0:T(8,128)(2,1)} %get-tuple-element.345), channel_id=1, source_target_pairs={{0,2},{2,0},{1,3},{3,1},{4,6},{6,4},{5,7},{7,5},{8,10},{10,8},{9,1... | collective-permute-start | bytes 1179656 | tf_op jit(solution)/shard_map/ppermute | solution.py:26
  228.2 158.8 %collective-permute-start.81 = (bf16[336,3072]{1,0:T(8,128)(2,1)}, bf16[336,3072]{1,0:T(8,128)(2,1)}, u32[]{:S(2)}, u32[]{:S(2)}) collective-permute-start(bf16[336,3072]{1,0:T(8,128)(2,1)} %pad_maximum_fusion.1), channel_id=1, source_target_pairs={{0,1},{1,0},{2,3},{3,2},{4,5},{5,4},{6,7},{7,6},{8,9},{9,8},{10,11... | collective-permute-start | bytes 6193160 | tf_op jit(solution)/shard_map/ppermute | solution.py:22
  286.9 18.2 %collective-permute-start.58 = (bf16[256,768]{1,0:T(8,128)(2,1)S(1)}, bf16[256,768]{1,0:T(8,128)(2,1)S(1)}, u32[]{:S(2)}, u32[]{:S(2)}) collective-permute-start(bf16[256,768]{1,0:T(8,128)(2,1)S(1)} %get-tuple-element.355), channel_id=1, source_target_pairs={{0,2},{2,0},{1,3},{3,1},{4,6},{6,4},{5,7},{7,5},{8,10},{10,8},{9,1... | collective-permute-start | bytes 1179656 | tf_op jit(solution)/shard_map/ppermute | solution.py:26
  288.7 81.0 %collective-permute-start.69 = (bf16[336,1536]{1,0:T(8,128)(2,1)}, bf16[336,1536]{1,0:T(8,128)(2,1)}, u32[]{:S(2)}, u32[]{:S(2)}) collective-permute-start(bf16[336,1536]{1,0:T(8,128)(2,1)} %pad_maximum_fusion.7), channel_id=1, source_target_pairs={{0,1},{1,0},{2,3},{3,2},{4,5},{5,4},{6,7},{7,6},{8,9},{9,8},{10,11... | collective-permute-start | bytes 3096584 | tf_op jit(solution)/shard_map/ppermute | solution.py:22
  321.2 17.6 %collective-permute-start.59 = (bf16[256,768]{1,0:T(8,128)(2,1)}, bf16[256,768]{1,0:T(8,128)(2,1)S(1)}, u32[]{:S(2)}, u32[]{:S(2)}) collective-permute-start(bf16[256,768]{1,0:T(8,128)(2,1)} %get-tuple-element.359), channel_id=1, source_target_pairs={{0,2},{2,0},{1,3},{3,1},{4,6},{6,4},{5,7},{7,5},{8,10},{10,8},{9,1... | collective-permute-start | bytes 1179656 | tf_op jit(solution)/shard_map/ppermute | solution.py:26
  323.4 132.0 %collective-permute-start.75 = (bf16[336,3072]{1,0:T(8,128)(2,1)}, bf16[336,3072]{1,0:T(8,128)(2,1)}, u32[]{:S(2)}, u32[]{:S(2)}) collective-permute-start(bf16[336,3072]{1,0:T(8,128)(2,1)} %pad_maximum_fusion), channel_id=1, source_target_pairs={{0,1},{1,0},{2,3},{3,2},{4,5},{5,4},{6,7},{7,6},{8,9},{9,8},{10,11... | collective-permute-start | bytes 6193160 | tf_op jit(solution)/shard_map/ppermute | solution.py:22
  382.0 14.8 %collective-permute-start.62 = (bf16[256,768]{1,0:T(8,128)(2,1)S(1)}, bf16[256,768]{1,0:T(8,128)(2,1)S(1)}, u32[]{:S(2)}, u32[]{:S(2)}) collective-permute-start(bf16[256,768]{1,0:T(8,128)(2,1)S(1)} %get-tuple-element.363), channel_id=1, source_target_pairs={{0,2},{2,0},{1,3},{3,1},{4,6},{6,4},{5,7},{7,5},{8,10},{10,8},{9,1... | collective-permute-start | bytes 1179656 | tf_op jit(solution)/shard_map/ppermute | solution.py:26
  387.0 56.0 %collective-permute-start.63 = (bf16[336,1536]{1,0:T(8,128)(2,1)}, bf16[336,1536]{1,0:T(8,128)(2,1)}, u32[]{:S(2)}, u32[]{:S(2)}) collective-permute-start(bf16[336,1536]{1,0:T(8,128)(2,1)} %pad_maximum_fusion.6), channel_id=1, source_target_pairs={{0,1},{1,0},{2,3},{3,2},{4,5},{5,4},{6,7},{7,6},{8,9},{9,8},{10,11... | collective-permute-start | bytes 3096584 | tf_op jit(solution)/shard_map/ppermute | solution.py:22
  392.0 33.6 %collective-permute-start.72 = (bf16[96,1536]{1,0:T(8,128)(2,1)}, bf16[96,1536]{1,0:T(8,128)(2,1)}, u32[]{:S(2)}, u32[]{:S(2)}) collective-permute-start(bf16[96,1536]{1,0:T(8,128)(2,1)} %add_convert_fusion.20), channel_id=1, source_target_pairs={{0,8},{1,5},{2,10},{3,7},{8,16},{9,1},{10,18},{11,3},{16,24},{17,9... | collective-permute-start | bytes 884744 | tf_op jit(solution)/shard_map/ppermute | solution.py:57
  409.4 30.5 %collective-permute-start.83 = (bf16[96,3072]{1,0:T(8,128)(2,1)}, bf16[96,3072]{1,0:T(8,128)(2,1)}, u32[]{:S(2)}, u32[]{:S(2)}) collective-permute-start(bf16[96,3072]{1,0:T(8,128)(2,1)} %add_convert_fusion.2), channel_id=1, source_target_pairs={{0,8},{1,5},{2,10},{3,7},{8,16},{9,1},{10,18},{11,3},{16,24},{17,9... | collective-permute-start | bytes 1769480 | tf_op jit(solution)/shard_map/ppermute | solution.py:57
  442.7 28.4 %collective-permute-start.84 = (bf16[96,3072]{1,0:T(8,128)(2,1)S(1)}, bf16[96,3072]{1,0:T(8,128)(2,1)S(1)}, u32[]{:S(2)}, u32[]{:S(2)}) collective-permute-start(bf16[96,3072]{1,0:T(8,128)(2,1)S(1)} %add_convert_fusion.1), channel_id=1, source_target_pairs={{0,8},{1,5},{2,10},{3,7},{8,16},{9,1},{10,18},{11,3},{16,24},{17,9... | collective-permute-start | bytes 1769480 | tf_op jit(solution)/shard_map/ppermute | solution.py:57
  487.1 19.1 %collective-permute-start.86 = (bf16[96,1536]{1,0:T(8,128)(2,1)}, bf16[96,1536]{1,0:T(8,128)(2,1)}, u32[]{:S(2)}, u32[]{:S(2)}) collective-permute-start(bf16[96,1536]{1,0:T(8,128)(2,1)} %select_convert_fusion.2), channel_id=1, source_target_pairs={{0,1},{1,0},{2,3},{3,2},{4,5},{5,4},{6,7},{7,6},{8,9},{9,8},{10,11... | collective-permute-start | bytes 884744 | tf_op jit(solution)/shard_map/ppermute | solution.py:22
  (226 other events, 1941.1 us)
